TPU v7x, 32 devices: a whole 2x2x4 slice. The times are simulated.
32 devices in a mesh: ctx: 16 (over z, x, core), fsdp: 2 (over y).
Axes of the slice: x: 2, y: 2, z: 4, core: 2. Of those that a mesh axis runs over, the one named last changes fastest.
Arguments:
- tokens: bfloat16 [2, 4096, 768], P('fsdp', 'ctx'), may hold values from -6 to 6
- cotangent: bfloat16 [2, 4096, 768], P('fsdp', 'ctx'), may hold values from -6 to 6
- lengths: int32 [2, 3], P('fsdp'), may hold values from 1 to 2048, 4096 in all within a row
- deal: int32 [2, 32], P('fsdp'), may hold values from 0 to 31, each once within a row
- joint_projection: bfloat16 [768, 2304], P('fsdp'), may hold values from -0.21875 to 0.21875
- output_projection: bfloat16 [768, 768], P('fsdp'), may hold values from -3 to 3
- expand_weight: bfloat16 [768, 2304], P('fsdp'), may hold values from -0.21875 to 0.21875
- contract_weight: bfloat16 [1152, 768], P('fsdp'), may hold values from -0.1875 to 0.1875
- gain_first: bfloat16 [768], P('fsdp'), may hold values from 0.099609375 to 1.8984375
- gain_second: bfloat16 [768], P('fsdp'), may hold values from 0.099609375 to 1.8984375
Outputs:
- output: bfloat16 [2, 4096, 768], P('fsdp', 'ctx')
- input_grad: bfloat16 [2, 4096, 768], P('fsdp', 'ctx')
- joint_grad: float32 [768, 2304], P('ctx')
- output_grad: float32 [768, 768], P('ctx')
- expand_grad: float32 [768, 2304], P('ctx')
- contract_grad: float32 [1152, 768], P('ctx')
- gain_first_grad: float32 [768], P('ctx')
- gain_second_grad: float32 [768], P('ctx')
Inputs may be any that keep to these rules, and one draw needn't show every extreme that they name: Each row of 3 lengths sums to 4096, and its longest is exactly 2048. Each row deal[g, :] is a permutation of the 32 blocks of a group.
All inputs are finite; a program needn't handle non-finite values.
Results may differ from a plain program's by a relative error of at most 0.029.
Values may be sent and summed in bfloat16 or wider, within the bound.
A program may use at most 192 MiB of HBM per device.

v0:
```python
import functools
import math

import jax
import jax.numpy as jnp
import numpy as np
from jax import lax
from jax.experimental import pallas as pl
from jax.experimental.pallas import tpu as pltpu
from jax.sharding import PartitionSpec as P

FF = 1152
HEADS = 12
HEAD_DIM = 64
BLOCK = 128
PLANES = 4
HD = HEAD_DIM
HALF = HEAD_DIM // 2
HP = HEADS // PLANES
QW = HP * HEAD_DIM
rope_base = 160000.0
norm_eps = 1e-05
MASKED = -1e30


def ends_of(lengths_ref, count):
    ends, total = [], 0
    for i in range(count):
        total = total + lengths_ref[0, i]
        ends.append(total)
    return ends


def span_of(index, ends):
    begin, end = jnp.zeros_like(index), jnp.full_like(index, ends[0])
    for before, after in zip(ends[:-1], ends[1:]):
        begin = jnp.where(index >= before, before, begin)
        end = jnp.where(index >= before, after, end)
    return begin, end


def head_rows(x, head):
    rows = lax.broadcasted_iota(jnp.int32, x.shape, 0)
    return jnp.where((rows >= head * HD) & (rows < (head + 1) * HD), x, jnp.zeros_like(x))


def query_block(n, b, T, ends):
    S = n // PLANES
    me = lax.axis_index("ctx")
    base = (lax.rem(me // S + PLANES - b, PLANES) * S + lax.rem(me, S)) * T
    low_begin, low_end = span_of(base, ends)
    high_begin, high_end = span_of(base + T - 1, ends)
    low, high = low_begin // T, (high_end + T - 1) // T
    full_low = jnp.clip((high_begin + T - 1) // T, low, high)
    full_high = jnp.clip(low_end // T, full_low, high)
    begin, end = span_of(base + lax.broadcasted_iota(jnp.int32, (8, T), 1), ends)
    return (low, full_low, full_high, high), begin[0:1], end[0:1]


def over_units(bounds, step, sizes):
    low, full_low, full_high, high = bounds
    in_groups(low, full_low, lambda u: step(u, True), sizes[-2:])
    in_groups(full_low, full_high, lambda u: step(u, False), sizes)
    in_groups(full_high, high, lambda u: step(u, True), sizes[-2:])


def in_groups(begin, end, step, sizes):
    for size in sizes:
        count = (end - begin) // size

        def some(i, carry, size=size, begin=begin):
            for e in range(size):
                step(begin + size * i + e)
            return carry

        lax.fori_loop(0, count, some, 0)
        begin = begin + size * count


def fwd_kernel(n, count, lengths_ref, qt_ref, kv_ref, ot_ref, lowt_ref, lse_ref, values, scores, top, total, acc):
    units, T, _ = kv_ref.shape
    ends = ends_of(lengths_ref, count)

    def flip(u, carry):
        values[u] = kv_ref[u, :, 128:].T
        return carry

    lax.fori_loop(0, units, flip, 0, unroll=4)

    def one_query_block(b, carry):
        qt = qt_ref[b]
        qheads = [head_rows(qt, h) for h in range(HP)]
        bounds, q_start, q_end = query_block(n, b, T, ends)
        top[...] = jnp.full_like(top, MASKED)
        total[...] = jnp.zeros_like(total)
        acc[...] = jnp.zeros_like(acc)

        def score(u, masked):
            k = kv_ref[u, :, :QW]
            st = [jnp.dot(k, qheads[h], preferred_element_type=jnp.float32) for h in range(HP)]
            if masked:
                at = u * T + lax.broadcasted_iota(jnp.int32, (T, T), 0)
                allowed = (at >= q_start) & (at < q_end)
                st = [jnp.where(allowed, s, MASKED) for s in st]
            for h in range(HP):
                scores[u, h] = st[h]
                top[h] = jnp.maximum(top[h], jnp.max(st[h].reshape(T // 8, 8, T), axis=0))

        over_units(bounds, score, (2, 1))
        m = [jnp.max(top[h], axis=0, keepdims=True) for h in range(HP)]

        def gather(u):
            p = [jnp.exp(scores[u, h] - m[h]) for h in range(HP)]
            for h in range(HP):
                total[h] += jnp.sum(p[h].reshape(T // 8, 8, T), axis=0)
                rows = pl.ds(h * HD, HD)
                acc[rows, :] += jnp.dot(
                    values[u, pl.ds(HD + h * HD, HD), :], p[h].astype(jnp.bfloat16), preferred_element_type=jnp.float32
                )

        in_groups(bounds[0], bounds[3], gather, (4, 2, 1))
        for h in range(HP):
            rows = pl.ds(h * HD, HD)
            l = jnp.sum(total[h], axis=0, keepdims=True)
            o = acc[rows, :] / l
            ot_ref[b, rows, :] = o
            lowt_ref[b, rows, :] = o.astype(jnp.bfloat16)
            lse_ref[b, h : h + 1, :] = m[h] + jnp.log(l)
        return carry

    lax.fori_loop(0, qt_ref.shape[0], one_query_block, 0)


def attn_fwd(n, lengths, qt, kv):
    B, _, T = qt.shape
    U = kv.shape[0]
    sm, vm = pl.BlockSpec(memory_space=pltpu.SMEM), pl.BlockSpec(memory_space=pltpu.VMEM)
    return pl.pallas_call(
        functools.partial(fwd_kernel, n, lengths.shape[1]),
        out_shape=(
            jax.ShapeDtypeStruct((B, QW, T), jnp.float32),
            jax.ShapeDtypeStruct((B, QW, T), jnp.bfloat16),
            jax.ShapeDtypeStruct((B, 8, T), jnp.float32),
        ),
        in_specs=[sm, vm, vm],
        out_specs=(vm, vm, vm),
        scratch_shapes=[
            pltpu.VMEM((U, 256, T), jnp.bfloat16),
            pltpu.VMEM((U, HP, T, T), jnp.float32),
            pltpu.VMEM((HP, 8, T), jnp.float32),
            pltpu.VMEM((HP, 8, T), jnp.float32),
            pltpu.VMEM((QW, T), jnp.float32),
        ],
        compiler_params=pltpu.CompilerParams(vmem_limit_bytes=60 << 20),
    )(lengths, qt, kv)


def bwd_kernel(n, count, lengths_ref, qt_ref, kv_ref, ot_ref, lse_ref, gt_ref, dqt_ref, dkv_ref, keys, dk, dv, dq):
    units, T, _ = kv_ref.shape
    ends = ends_of(lengths_ref, count)

    def flip(u, carry):
        keys[u] = kv_ref[u, :, :256].T
        dk[u] = jnp.zeros_like(dk[u])
        dv[u] = jnp.zeros_like(dv[u])
        return carry

    lax.fori_loop(0, units, flip, 0, unroll=4)

    def one_query_block(b, carry):
        qt, gt = qt_ref[b], gt_ref[b]
        zero = jnp.zeros((HD, T), jnp.bfloat16)
        qheads = [head_rows(qt, h) for h in range(HP)]
        gheads = [head_rows(gt, h) for h in range(HP)]
        gpad = [jnp.concatenate([zero, x], axis=0) for x in gheads]
        lanes = lax.broadcasted_iota(jnp.int32, (T, 256), 1) // HD
        q, g = jnp.concatenate([qt, zero], axis=0).T, jnp.concatenate([zero, gt], axis=0).T
        q = jnp.concatenate([jnp.where(lanes == h, q, jnp.zeros_like(q)) for h in range(HP)], axis=0)
        g = jnp.concatenate([jnp.where(lanes == h + 1, g, jnp.zeros_like(g)) for h in range(HP)], axis=0)
        bounds, q_start, q_end = query_block(n, b, T, ends)
        prod = gt.astype(jnp.float32) * ot_ref[b]
        delta = [jnp.sum(prod[h * HD : (h + 1) * HD], axis=0, keepdims=True) for h in range(HP)]
        lse = [lse_ref[b, h : h + 1, :] for h in range(HP)]
        dq[...] = jnp.zeros_like(dq)

        def one_unit(u, masked):
            k, v = kv_ref[u, :, :QW], kv_ref[u, :, 128:]
            st = [jnp.dot(k, qheads[h], preferred_element_type=jnp.float32) for h in range(HP)]
            dp = [jnp.dot(v, gpad[h], preferred_element_type=jnp.float32) for h in range(HP)]
            st = [st[h] - lse[h] for h in range(HP)]
            if masked:
                at = u * T + lax.broadcasted_iota(jnp.int32, (T, T), 0)
                allowed = (at >= q_start) & (at < q_end)
                st = [jnp.where(allowed, s, MASKED) for s in st]
            p = [jnp.exp(s) for s in st]
            ds = [(p[h] * (dp[h] - delta[h])).astype(jnp.bfloat16) for h in range(HP)]
            p = [x.astype(jnp.bfloat16) for x in p]
            dv[u] += jnp.dot(jnp.concatenate(p, axis=1), g, preferred_element_type=jnp.float32)
            dk[u] += jnp.dot(jnp.concatenate(ds, axis=1), q, preferred_element_type=jnp.float32)
            for h in range(HP):
                rows = pl.ds(h * HD, HD)
                dq[rows, :] += jnp.dot(keys[u, rows, :], ds[h], preferred_element_type=jnp.float32)

        over_units(bounds, one_unit, (4, 2, 1))
        dqt_ref[b] = dq[...] * (HD**-0.5)
        return carry

    lax.fori_loop(0, qt_ref.shape[0], one_query_block, 0)

    def out(u, carry):
        dkv_ref[u, :, :128] = dk[u, :, :128].astype(jnp.bfloat16)
        dkv_ref[u, :, 128:256] = (dk[u, :, 128:] + dv[u, :, :128]).astype(jnp.bfloat16)
        dkv_ref[u, :, 256:] = dv[u, :, 128:].astype(jnp.bfloat16)
        return carry

    lax.fori_loop(0, units, out, 0, unroll=2)


def attn_bwd(n, lengths, qt, kv, ot, lse, gt):
    B, _, T = qt.shape
    U = kv.shape[0]
    sm, vm = pl.BlockSpec(memory_space=pltpu.SMEM), pl.BlockSpec(memory_space=pltpu.VMEM)
    return pl.pallas_call(
        functools.partial(bwd_kernel, n, lengths.shape[1]),
        out_shape=(jax.ShapeDtypeStruct((B, QW, T), jnp.float32), jax.ShapeDtypeStruct((U, T, 2 * QW), jnp.bfloat16)),
        in_specs=[sm] + [vm] * 5,
        out_specs=(vm, vm),
        scratch_shapes=[
            pltpu.VMEM((U, 256, T), jnp.bfloat16),
            pltpu.VMEM((U, T, 256), jnp.float32),
            pltpu.VMEM((U, T, 256), jnp.float32),
            pltpu.VMEM((QW, T), jnp.float32),
        ],
        compiler_params=pltpu.CompilerParams(vmem_limit_bytes=60 << 20),
    )(lengths, qt, kv, ot, lse, gt)
def front_kernel(
    n,
    groups,
    count,
    lengths_ref,
    tokens_ref,
    joint_ref,
    gain_one_ref,
    gain_two_ref,
    out_hbm,
    exp_hbm,
    con_hbm,
    first_ref,
    qt_ref,
    kv_ref,
    joint_t_out,
    turn_ref,
    gains_ref,
    out_all,
    exp_all,
    con_ref,
    held,
    t_sems,
    cols,
    cols_all,
    gain_held,
    g_sems,
    kv_own,
    kv_sems,
    own_sems,
    w_sems,
    w_local,
    joint_rows,
    out_held,
    exp_held,
    con_held,
):
    bf, f32 = jnp.bfloat16, jnp.float32
    S = n // PLANES
    S2 = S // 2
    T, D = tokens_ref.shape
    me, group = lax.axis_index("ctx"), lax.axis_index("fsdp")
    plane, side = me // S, lax.rem(me, S)
    s2, core = side // 2, lax.rem(side, 2)

    def at(p, a, c, g):
        return (p * S + a * 2 + c, g)

    def side_peer(k):
        return at(plane, lax.rem(s2 + k, S2), core, group)

    def group_peer(k):
        return at(plane, s2, core, lax.rem(group + k, groups))

    core_peer = at(plane, s2, 1 - core, group)

    def remote(source, target, sems, index, device):
        return pltpu.make_async_remote_copy(
            src_ref=source,
            dst_ref=target,
            send_sem=sems.at[0, index],
            recv_sem=sems.at[1, index],
            device_id=device,
            device_id_type=pl.DeviceIdType.MESH,
        )

    barrier = pltpu.get_barrier_semaphore()

    def greet(device):
        pl.semaphore_signal(barrier, inc=1, device_id=device, device_id_type=pl.DeviceIdType.MESH)

    for k in range(1, PLANES):
        greet(at(lax.rem(plane + k, PLANES), s2, core, group))
    for k in range(1, S2):
        greet(side_peer(k))
    for k in range(1, groups):
        greet(group_peer(k))
    greet(core_peer)
    pl.semaphore_wait(barrier, PLANES - 1 + S2 - 1 + groups - 1 + 1)

    def up(p):
        return remote(held.at[p], held.at[p], t_sems, p, at(plane + 1, s2, core, group))

    def down(p):
        return remote(held.at[p], held.at[p], t_sems, PLANES + p, at(plane - 1, s2, core, group))

    held[plane] = tokens_ref[...]

    @pl.when(plane < PLANES - 1)
    def _():
        up(plane).start()

    @pl.when(plane > 0)
    def _():
        down(plane).start()

    pair = 2 * QW
    for part in range(3):
        window = joint_ref[:, pl.ds(pl.multiple_of(part * D + plane // 2 * pair, 128), pair)].T
        chosen = jnp.where(lax.rem(plane, 2) == 0, window[:QW].astype(f32), window[QW:].astype(f32))
        half = 3 * QW // 2
        low, high = part * QW, (part + 1) * QW
        for c in range(2):
            begin, end = max(low, c * half), min(high, (c + 1) * half)
            if begin < end:
                cols[c, begin - c * half : end - c * half] = chosen[begin - low : end - low].astype(bf)
    gain_held[group] = jnp.zeros_like(gain_held[group])
    gain_held[group, 0:1] = gain_one_ref[...].astype(f32).reshape(1, -1)
    gain_held[group, 1:2] = gain_two_ref[...].astype(f32).reshape(1, -1)
    col_moves = [
        remote(cols.at[core], cols_all.at[group, core], g_sems, k - 1, group_peer(k)) for k in range(1, groups)
    ]
    col_hands = []
    for k in range(1, groups):
        came = cols_all.at[lax.rem(group + groups - k, groups), core]
        col_hands.append(remote(came, came, g_sems, 2 * (groups - 1) + k - 1, core_peer))
    gain_moves = [
        remote(gain_held.at[group], gain_held.at[group], g_sems, groups - 1 + k - 1, group_peer(k))
        for k in range(1, groups)
    ]
    for copy in gain_moves + col_moves:
        copy.start()
    cols_all[group] = cols[...]

    weights = [(out_hbm, out_all, out_held), (exp_hbm, exp_all, exp_held)]
    part = core if con_hbm.shape[0] == 2 else 0
    w_in = [pltpu.make_async_copy(con_hbm.at[part], con_held, w_local.at[0, len(weights)])]
    w_own = [pltpu.make_async_copy(con_held, con_ref, w_local.at[1, len(weights)])]
    w_first, w_second = [], []
    for i, (source, target, bounce) in enumerate(weights):
        w_in.append(pltpu.make_async_copy(source, bounce, w_local.at[0, i]))
        w_own.append(pltpu.make_async_copy(bounce, target.at[group], w_local.at[1, i]))
        for k in range(1, groups):
            index = (i * (groups - 1) + k - 1) * 2
            w_first.append(remote(source.at[core], target.at[group, core], w_sems, index, group_peer(k)))
            came = lax.rem(group + groups - k, groups)
            w_second.append(remote(target.at[came, core], target.at[came, core], w_sems, index + 1, core_peer))
    for copy in w_in:
        copy.start()
    for copy in w_first:
        copy.start()

    ends = ends_of(lengths_ref, count)
    row = lax.broadcasted_iota(jnp.int32, (HALF, T), 0)
    frequencies = jnp.zeros((HALF, T), f32)
    for i in range(HALF):
        frequencies = jnp.where(row == i, float(np.float32(rope_base ** (-2.0 * i / HEAD_DIM))), frequencies)
    for j in range(PLANES):
        base = (lax.rem(plane + PLANES - j, PLANES) * S + side) * T
        index = base + lax.broadcasted_iota(jnp.int32, (8, T), 1)
        begin, _ = span_of(index, ends)
        angles = (index - begin)[0:1].astype(f32) * frequencies
        turn_ref[j, :HALF] = jnp.cos(angles)
        turn_ref[j, HALF:] = jnp.sin(angles)

    strip = 64

    def kv_unit(p, a, c):
        return p * S + a * 2 + c

    def side_kv(j, k):
        p = lax.rem(plane + PLANES - j, PLANES)
        return remote(kv_own.at[j], kv_ref.at[kv_unit(p, s2, core)], kv_sems, j * (2 * S2 - 1) + k - 1, side_peer(k))

    def core_kv(j, k):
        p = lax.rem(plane + PLANES - j, PLANES)
        unit = kv_unit(p, lax.rem(s2 + S2 - k, S2), core)
        source = kv_own.at[j] if k == 0 else kv_ref.at[unit]
        return remote(source, kv_ref.at[unit], kv_sems, j * (2 * S2 - 1) + S2 - 1 + k, core_peer)

    def own_kv(j):
        p = lax.rem(plane + PLANES - j, PLANES)
        return pltpu.make_async_copy(kv_own.at[j], kv_ref.at[kv_unit(p, s2, core)], own_sems.at[j])

    def process(p):
        j = lax.rem(plane + PLANES - p, PLANES)

        def norm(i, carry):
            rows = pl.ds(pl.multiple_of(i * strip, strip), strip)
            values = held[p, rows].astype(f32)
            centred = values - jnp.mean(values, axis=-1, keepdims=True)
            spread = jnp.mean(centred * centred, axis=-1, keepdims=True)
            first_ref[j, rows] = (centred * lax.rsqrt(spread + norm_eps) * gains_ref[0:1]).astype(bf)
            return carry

        lax.fori_loop(0, T // strip, norm, 0)
        mixed = lax.dot_general(
            joint_t_out[: 3 * QW], first_ref[j], (((1,), (1,)), ((), ())), preferred_element_type=f32
        )
        cos, sin = turn_ref[j, :HALF], turn_ref[j, HALF:]
        turned = []
        for h in range(2 * HP):
            upper, lower = mixed[h * HD : h * HD + HALF], mixed[h * HD + HALF : (h + 1) * HD]
            turned += [upper * cos - lower * sin, lower * cos + upper * sin]
        q = jnp.concatenate(turned[: 2 * HP], axis=0).astype(bf)
        qt_ref[j] = (q.astype(f32) * HEAD_DIM**-0.5).astype(bf)
        kv_own[j] = jnp.concatenate(turned[2 * HP :] + [mixed[2 * QW :]], axis=0).T.astype(bf)
        for k in range(1, S2):
            side_kv(j, k).start()
        core_kv(j, 0).start()
        own_kv(j).start()

    def hand_on(t):
        @pl.when(plane >= t)
        def _():
            up(plane - t).wait_recv()

            @pl.when(plane < PLANES - 1)
            def _():
                up(plane - t).start()

        @pl.when(plane + t < PLANES)
        def _():
            down(plane + t).wait_recv()

            @pl.when(plane > 0)
            def _():
                down(plane + t).start()

    def process_arrived(t):
        below = jnp.where(plane >= t, 1, 0)
        above = jnp.where(plane + t < PLANES, 1, 0)

        def arrived(i, carry):
            process(jnp.where(i < below, plane - t, plane + t))
            return carry

        lax.fori_loop(0, below + above, arrived, 0)

    hand_on(1)
    for copy in gain_moves:
        copy.wait()
    share = D // groups
    total = jnp.zeros((8, D), f32)
    for g in range(groups):
        rows = lax.broadcasted_iota(jnp.int32, (share, D), 0)
        lanes = lax.broadcasted_iota(jnp.int32, (share, D), 1)
        place = jnp.where(lanes == rows + g * share, 1.0, 0.0).astype(bf)
        total = total + jnp.dot(gain_held[g].astype(bf), place, preferred_element_type=f32)
    gains_ref[...] = total
    for copy, hand in zip(col_moves, col_hands):
        copy.wait()
        hand.start()
    for copy in w_in:
        copy.wait()
    for copy in w_own:
        copy.start()
    for copy in col_hands:
        copy.wait()
    width = joint_t_out.shape[0]
    for g in range(groups):
        whole = jnp.concatenate([cols_all[g, 0], cols_all[g, 1], jnp.zeros((width - 3 * QW, share), bf)], axis=0)
        if share % 128 == 0:
            joint_t_out[:, g * share : (g + 1) * share] = whole
        else:
            joint_rows[g * share : (g + 1) * share] = whole.T
    if share % 128:
        for i in range(D // 128):
            joint_t_out[:, i * 128 : (i + 1) * 128] = joint_rows[i * 128 : (i + 1) * 128].T

    process(plane)
    process_arrived(1)
    hand_on(2)
    process_arrived(2)
    hand_on(3)
    for first_move, second_move in zip(w_first[: groups - 1], w_second):
        first_move.wait_recv()
        second_move.start()
    process_arrived(3)

    for j in range(PLANES):
        for k in range(1, S2):
            side_kv(j, k).wait_recv()
            core_kv(j, k).start()
    for first_move, second_move in zip(w_first[groups - 1 :], w_second[groups - 1 :]):
        first_move.wait_recv()
        second_move.start()

    for j in range(PLANES):
        own_kv(j).wait()
        for k in range(1, S2):
            side_kv(j, k).wait_send()
        for k in range(S2):
            core_kv(j, k).wait()
    for p in range(PLANES):

        @pl.when((plane < PLANES - 1) & (plane >= p))
        def _(p=p):
            up(p).wait_send()

        @pl.when((plane > 0) & (plane <= p))
        def _(p=p):
            down(p).wait_send()

    for copy in w_own:
        copy.wait()
    for first_move, second_move in zip(w_first, w_second):
        first_move.wait_send()
        second_move.wait()


def front(n, groups, lengths, tokens, joint_shard, gain_first, gain_second, out_w, exp_w, con_w):
    bf, f32 = jnp.bfloat16, jnp.float32
    S2 = n // PLANES // 2
    T, D = tokens.shape
    width = 3 * QW + 64
    share = D // groups
    any_, vm, sm = (pl.BlockSpec(memory_space=m) for m in (pl.ANY, pltpu.VMEM, pltpu.SMEM))
    sems = lambda count: pltpu.SemaphoreType.DMA((2, count))
    halves = lambda w: w.reshape(2, w.shape[0] // 2, w.shape[1])
    weights = [halves(w) for w in (out_w, exp_w)]
    con_w = con_w.reshape(2 if con_w.shape[0] % 32 == 0 else 1, -1, D)
    return pl.pallas_call(
        functools.partial(front_kernel, n, groups, lengths.shape[1]),
        out_shape=(
            jax.ShapeDtypeStruct((PLANES, T, D), bf),
            jax.ShapeDtypeStruct((PLANES, QW, T), bf),
            jax.ShapeDtypeStruct((n, T, 2 * QW), bf),
            jax.ShapeDtypeStruct((width, D), bf),
            jax.ShapeDtypeStruct((PLANES, 2 * HALF, T), f32),
            jax.ShapeDtypeStruct((8, D), f32),
            *[jax.ShapeDtypeStruct((groups, *w.shape), bf) for w in weights],
            jax.ShapeDtypeStruct(con_w.shape[1:], bf),
        ),
        in_specs=[sm, vm, vm, vm, vm, any_, any_, any_],
        out_specs=(vm, vm, any_, vm, vm, vm, any_, any_, any_),
        scratch_shapes=[
            pltpu.VMEM((PLANES, T, D), bf),
            sems(2 * PLANES),
            pltpu.VMEM((2, 3 * QW // 2, share), bf),
            pltpu.VMEM((groups, 2, 3 * QW // 2, share), bf),
            pltpu.VMEM((groups, 8, share), f32),
            sems(3 * (groups - 1)),
            pltpu.VMEM((PLANES, T, 2 * QW), bf),
            sems(PLANES * (2 * S2 - 1)),
            pltpu.SemaphoreType.DMA((PLANES,)),
            sems(2 * len(weights) * (groups - 1)),
            pltpu.SemaphoreType.DMA((2, len(weights) + 1)),
            pltpu.VMEM((D, width), bf),
            *[pltpu.VMEM(w.shape, bf) for w in weights],
            pltpu.VMEM(con_w.shape[1:], bf),
        ],
        compiler_params=pltpu.CompilerParams(collective_id=1, has_side_effects=True, vmem_limit_bytes=60 << 20),
    )(
        lengths,
        tokens,
        joint_shard,
        gain_first,
        gain_second,
        *weights,
        con_w,
    )


def middle_kernel(
    n,
    groups,
    low_ref,
    tokens_ref,
    cot_ref,
    gains_ref,
    out_hbm,
    exp_hbm,
    con_hbm,
    joint_hbm,
    *refs,
):
    con_got, refs = refs[: groups - 1], refs[groups - 1 :]
    (
        output_ref,
        grad_hidden_ref,
        gt_ref,
        y_keep,
        y_send,
        x_keep,
        x_send,
        z_keep,
        z_send_1,
        z_send_2,
        z_send_3,
        joint_near,
        out_w,
        exp_w,
        con_w,
        local_sems,
        c_sems,
        joint_shard,
        cols,
        cols_all,
        col_sems,
        joint_rows,
        att,
        a_sems,
        g_send,
        g_sems,
        hidden,
        second,
        branch,
        ga,
        act,
        gexp,
        acc,
        w_own,
        w_other,
        w_got,
        w_sems,
    ) = refs
    bf, f32 = jnp.bfloat16, jnp.float32
    S = n // PLANES
    S2 = S // 2
    T, D = tokens_ref.shape
    FFN = act.shape[1]
    me, group = lax.axis_index("ctx"), lax.axis_index("fsdp")
    plane, side = me // S, lax.rem(me, S)
    s2, core = side // 2, lax.rem(side, 2)

    def plane_peer(k):
        return (lax.rem(plane + k, PLANES) * S + side, group)

    core_peer = (plane * S + s2 * 2 + 1 - core, group)

    def group_peer(k):
        return (me, lax.rem(group + k, groups))


    def remote(source, target, sems, index, device):
        return pltpu.make_async_remote_copy(
            src_ref=source,
            dst_ref=target,
            send_sem=sems.at[0, index],
            recv_sem=sems.at[1, index],
            device_id=device,
            device_id_type=pl.DeviceIdType.MESH,
        )

    ff_share = con_hbm.shape[0]
    split = ff_share % 32 == 0

    def rows_of(g):
        return pl.ds(pl.multiple_of(g * ff_share, 16), ff_share)

    def half_of(g):
        if not split:
            return rows_of(g)
        half = ff_share // 2
        return pl.ds(pl.multiple_of(g * ff_share + core * half, 16), half)

    came = [half_of(lax.rem(group + groups - k, groups)) for k in range(1, groups)]
    con_hands = [remote(con_got[k], con_w.at[came[k]], c_sems, k, core_peer) for k in range(groups - 1)]
    con_local = [
        pltpu.make_async_copy(con_got[k], con_w.at[came[k]], local_sems.at[3 + k]) for k in range(groups - 1)
    ]
    local = [
        pltpu.make_async_copy(source, target, local_sems.at[i])
        for i, (source, target) in enumerate([(con_hbm, con_w.at[rows_of(group)]), (out_hbm, out_w), (exp_hbm, exp_w)])
    ]
    joint_local = pltpu.make_async_copy(joint_hbm, joint_shard, local_sems.at[3 + groups - 1])
    for copy in [joint_local] + local + con_local:
        copy.start()
    barrier = pltpu.get_barrier_semaphore()
    for k in range(1, PLANES):
        pl.semaphore_signal(barrier, inc=1, device_id=plane_peer(k), device_id_type=pl.DeviceIdType.MESH)
    pl.semaphore_signal(barrier, inc=1, device_id=core_peer, device_id_type=pl.DeviceIdType.MESH)
    for k in range(1, groups):
        pl.semaphore_signal(barrier, inc=1, device_id=group_peer(k), device_id_type=pl.DeviceIdType.MESH)
    pl.semaphore_wait(barrier, PLANES + groups - 1)

    home = [remote(low_ref.at[j], att.at[plane], a_sems, j - 1, plane_peer(PLANES - j)) for j in range(1, PLANES)]
    for copy in home + (con_hands if split else []):
        copy.start()
    att[plane] = low_ref[0]

    joint_local.wait()
    pair = 2 * QW
    for part in range(3):
        window = joint_shard[:, pl.ds(pl.multiple_of(part * D + plane // 2 * pair, 128), pair)].T
        chosen = jnp.where(lax.rem(plane, 2) == 1, window[:QW].astype(f32), window[QW:].astype(f32))
        half = 3 * QW // 2
        low, high = part * QW, (part + 1) * QW
        for c in range(2):
            begin, end = max(low, c * half), min(high, (c + 1) * half)
            if begin < end:
                cols[c, begin - c * half : end - c * half] = chosen[begin - low : end - low].astype(bf)
    col_moves = [
        remote(cols.at[core], cols_all.at[group, core], col_sems, k - 1, group_peer(k)) for k in range(1, groups)
    ]
    col_hands = []
    for k in range(1, groups):
        col_came = cols_all.at[lax.rem(group + groups - k, groups), core]
        col_hands.append(remote(col_came, col_came, col_sems, groups - 1 + k - 1, core_peer))
    for copy in col_moves:
        copy.start()
    cols_all[group] = cols[...]

    def nt(a, b):
        return lax.dot_general(a, b, (((1,), (1,)), ((), ())), preferred_element_type=f32)

    chunk = 384
    cot = cot_ref[...]
    local[0].wait()
    for copy in con_local + (con_hands if split else []):
        copy.wait()
    for c in range(0, FFN, chunk):
        ga[:, c : c + chunk] = nt(cot, con_w[c : c + chunk])
    local[1].wait()
    for copy in home:
        copy.wait()
    attended = att[...].reshape(D, T)
    hidden[...] = tokens_ref[...].astype(f32) + jnp.dot(attended.T, out_w[...], preferred_element_type=f32)

    strip = 64

    for copy, hand in zip(col_moves, col_hands):
        copy.wait()
        hand.start()

    def norm(i, carry):
        rows = pl.ds(pl.multiple_of(i * strip, strip), strip)
        values = hidden[rows]
        centred = values - jnp.mean(values, axis=-1, keepdims=True)
        spread = jnp.mean(centred * centred, axis=-1, keepdims=True)
        second[rows] = (centred * lax.rsqrt(spread + norm_eps) * gains_ref[1:2]).astype(bf)
        return carry

    lax.fori_loop(0, T // strip, norm, 0)
    local[2].wait()
    for c in range(0, FFN, chunk):
        cols, gate_cols = slice(c, c + chunk), slice(FFN + c, FFN + c + chunk)
        inner = jnp.dot(second[...], exp_w[:, cols], preferred_element_type=f32)
        gate = jnp.dot(second[...], exp_w[:, gate_cols], preferred_element_type=f32)
        share = 0.5 * (1.0 + lax.erf(inner * (0.5**0.5)))
        bent = inner * share
        act[:, cols] = (bent * gate).astype(bf)
        grad = ga[:, cols]
        slope = share + inner * jnp.exp(-0.5 * inner * inner) * ((2.0 * math.pi) ** -0.5)
        gexp[:, cols] = (grad * gate * slope).astype(bf)
        gexp[:, gate_cols] = (grad * bent).astype(bf)
    output_ref[...] = (hidden[...] + jnp.dot(act[...], con_w[...], preferred_element_type=f32)).astype(bf)
    acc[:T] = nt(gexp[...], exp_w[...])

    def norm_back(i, total):
        rows = pl.ds(pl.multiple_of(i * strip, strip), strip)
        values = hidden[rows]
        centred = values - jnp.mean(values, axis=-1, keepdims=True)
        scale = lax.rsqrt(jnp.mean(centred * centred, axis=-1, keepdims=True) + norm_eps)
        normal = centred * scale
        grad = acc[rows]
        total = total + jnp.sum(grad * normal, axis=0, keepdims=True)
        grad = grad * gains_ref[1:2]
        grad = grad - jnp.mean(grad, axis=-1, keepdims=True) - normal * jnp.mean(grad * normal, axis=-1, keepdims=True)
        back = cot_ref[rows].astype(f32) + grad * scale
        grad_hidden_ref[rows] = back
        branch[rows] = back.astype(bf)
        return total

    total = lax.fori_loop(0, T // strip, norm_back, jnp.zeros((1, D), f32))
    gain_two = jnp.broadcast_to(total, (8, D))
    for p in range(PLANES):
        g_send[p] = nt(out_w[p * QW : (p + 1) * QW], branch[...]).astype(bf)
    away = [
        remote(g_send.at[lax.rem(plane + k, PLANES)], gt_ref.at[k], g_sems, k - 1, plane_peer(k))
        for k in range(1, PLANES)
    ]
    for copy in away:
        copy.start()
    gt_ref[0] = g_send[plane]

    for copy in col_hands:
        copy.wait()
    share = D // groups
    for g in range(groups):
        whole = jnp.concatenate([cols_all[g, 0], cols_all[g, 1]], axis=0)
        if share % 128 == 0:
            joint_near[:, g * share : (g + 1) * share] = whole
        else:
            joint_rows[g * share : (g + 1) * share] = whole.T
    if share % 128:
        for i in range(D // 128):
            joint_near[:, i * 128 : (i + 1) * 128] = joint_rows[i * 128 : (i + 1) * 128].T

    sent = []

    def place(rows, offset, height):
        for target, parity in ((w_other, 1 - core), (w_own, core)):

            def body(m, carry):
                if rows % 8:
                    pair = acc[pl.ds(pl.multiple_of(2 * m * rows, 8), 2 * rows)]
                    value = jnp.where(parity == 0, pair[:rows], pair[rows:])
                else:
                    value = acc[pl.ds(pl.multiple_of((2 * m + parity) * rows, 8), rows)]
                if height > rows:
                    rest = jnp.zeros((height - rows - 8, D), f32)
                    value = jnp.concatenate([value, gain_two, rest], axis=0)
                value = value.astype(bf)
                target[m, offset : offset + height] = value
                return carry

            lax.fori_loop(0, n // 2, body, 0)
        part = pl.ds(offset, height)
        sent.append(remote(w_other.at[:, part], w_got.at[:, part], w_sems, len(sent), core_peer))
        sent[-1].start()

    rows = D // n
    wide = 2 * FFN // D
    for c in range(0, FFN, chunk):
        acc[c : c + chunk] = jnp.dot(act[:, c : c + chunk].T, cot_ref[...], preferred_element_type=f32)
    used = (1 + wide) * rows
    place(FFN // n, used, w_own.shape[1] - used)
    second_t = second[...].T
    for i in range(wide):
        acc[:D] = jnp.dot(second_t, gexp[:, i * D : (i + 1) * D], preferred_element_type=f32)
        place(rows, (1 + i) * rows, rows)
    acc[:D] = jnp.dot(attended, branch[...], preferred_element_type=f32)
    place(rows, 0, rows)

    for copy in sent:
        copy.wait()
    height = y_keep.shape[2]
    third = lambda g, i: pl.ds(pl.multiple_of((3 * g + i) * height, 16), height)

    def summed(m, part):
        return (w_own[m, part].astype(f32) + w_got[m, part].astype(f32)).astype(bf)

    def each(count, body):
        def step(i, carry):
            body(i)
            return carry

        lax.fori_loop(0, count, step, 0)

    for k in range(groups):
        g = lax.rem(group + k, groups)

        def first(m, k=k, g=g):
            (y_send.at[k - 1] if k else y_keep)[m // S2, lax.rem(m, S2)] = summed(m, third(g, 0))

        each(PLANES * S2, first)
    for k in range(S2):
        a = lax.rem(s2 + k, S2)

        def second_part(i, k=k, a=a):
            p, g = i // groups, lax.rem(i, groups)
            (x_send.at[k - 1] if k else x_keep)[p, g] = summed(p * S2 + a, third(g, 1))

        each(PLANES * groups, second_part)
    z_parts = [z_keep, z_send_1, z_send_2, z_send_3]
    for k in range(PLANES):
        p = lax.rem(plane + k, PLANES)

        def third_part(i, k=k, p=p):
            a, g = i // groups, lax.rem(i, groups)
            z_parts[k][a, g] = summed(p * S2 + a, third(g, 2))

        each(S2 * groups, third_part)
    for copy in away:
        copy.wait()


def middle(n, groups, lowt, tokens, cotangent, gains, out_w, exp_w, con_w, joint_shard, con_got):
    bf, f32 = jnp.bfloat16, jnp.float32
    S2 = n // PLANES // 2
    T, D = tokens.shape
    ffn = con_w.shape[0] * groups
    used = (D + 2 * ffn + ffn) // n + 8
    height = -(-used // (groups * 48)) * 16
    any_, vm = pl.BlockSpec(memory_space=pl.ANY), pl.BlockSpec(memory_space=pltpu.VMEM)
    sems = lambda count: pltpu.SemaphoreType.DMA((2, count))
    shape = lambda *s: jax.ShapeDtypeStruct(s, bf)
    half = (n // 2, 3 * groups * height, D)
    return pl.pallas_call(
        functools.partial(middle_kernel, n, groups),
        out_shape=(
            shape(T, D),
            jax.ShapeDtypeStruct((T, D), f32),
            shape(PLANES, QW, T),
            shape(PLANES, S2, height, D),
            shape(groups - 1, PLANES, S2, height, D),
            shape(PLANES, groups, height, D),
            shape(S2 - 1, PLANES, groups, height, D),
            shape(S2, groups, height, D),
            *[shape(S2, groups, height, D)] * (PLANES - 1),
            shape(3 * QW, D),
        ),
        in_specs=[vm, vm, vm, vm, any_, any_, any_, any_] + [any_] * (groups - 1),
        out_specs=tuple([vm] * 12),
        scratch_shapes=[
            pltpu.VMEM(out_w.shape, bf),
            pltpu.VMEM(exp_w.shape, bf),
            pltpu.VMEM((ffn, D), bf),
            pltpu.SemaphoreType.DMA((4 + groups - 1,)),
            sems(groups - 1),
            pltpu.VMEM(joint_shard.shape, bf),
            pltpu.VMEM((2, 3 * QW // 2, D // groups), bf),
            pltpu.VMEM((groups, 2, 3 * QW // 2, D // groups), bf),
            sems(2 * (groups - 1)),
            pltpu.VMEM((D, 3 * QW), bf),
            pltpu.VMEM((PLANES, QW, T), bf),
            sems(PLANES - 1),
            pltpu.VMEM((PLANES, QW, T), bf),
            sems(PLANES - 1),
            pltpu.VMEM((T, D), f32),
            pltpu.VMEM((T, D), bf),
            pltpu.VMEM((T, D), bf),
            pltpu.VMEM((T, ffn), f32),
            pltpu.VMEM((T, ffn), bf),
            pltpu.VMEM((T, 2 * ffn), bf),
            pltpu.VMEM((ffn, D), f32),
            pltpu.VMEM(half, bf),
            pltpu.VMEM(half, bf),
            pltpu.VMEM(half, bf),
            sems(2 + 2 * ffn // D),
        ],
        compiler_params=pltpu.CompilerParams(collective_id=2, has_side_effects=True, vmem_limit_bytes=60 << 20),
    )(lowt, tokens, cotangent, gains, out_w, exp_w, con_w, joint_shard, *con_got)


def tail_kernel(
    n,
    groups,
    deal_ref,
    dq_hbm,
    dkv_hbm,
    turn_ref,
    gains_ref,
    joint_hbm,
    joint_t_hbm,
    joint_near_hbm,
    first_hbm,
    tokens_hbm,
    grad_hidden_hbm,
    y_keep_hbm,
    y_got_hbm,
    x_keep_hbm,
    x_got_hbm,
    z_keep_hbm,
    z_got_1,
    z_got_2,
    z_got_3,
    d_got,
    w_all,
    jq_all,
    jk_all,
    joint_rows,
    joint_t,
    joint_near,
    first,
    tokens,
    grad_hidden,
    y_keep,
    y_got,
    x_keep,
    x_got,
    z_keep,
    z_came,
    local_sems,
    dq_ref,
    kv_own,
    own_sems,
    kv_near,
    kv_send,
    kv_far,
    kv_sems,
    mixed,
    mixed_got,
    mixed_send_sems,
    mixed_recv_sems,
    part,
    part_got,
    part_send_sems,
    part_recv_sems,
    j_acc,
    jq,
    jq_core,
    jq_side,
    jq_plane,
    jk,
    jk_core,
    jk_side,
    jk_plane,
    j_sems,
    x1_got,
    y2_got,
    y3_got,
    z1_got,
    z1_sems,
    x3_got,
    w_plane,
    w_plane_got,
    w_sems,
    d_send,
    d_mid,
    d_back,
    d_sems,
    row_sems,
    row_local,
):
    bf, f32 = jnp.bfloat16, jnp.float32
    S = n // PLANES
    S2 = S // 2
    T, D = tokens.shape
    me, group = lax.axis_index("ctx"), lax.axis_index("fsdp")
    plane, side = me // S, lax.rem(me, S)
    s2, core = side // 2, lax.rem(side, 2)
    MESH = pl.DeviceIdType.MESH

    def at(p, a, c, g):
        return (p * S + a * 2 + c, g)

    def plane_peer(k):
        return at(lax.rem(plane + k, PLANES), s2, core, group)

    def side_peer(k):
        return at(plane, lax.rem(s2 + k, S2), core, group)

    def group_peer(k):
        return at(plane, s2, core, lax.rem(group + k, groups))

    core_peer = at(plane, s2, 1 - core, group)

    def send(source, target, send_sem, recv_sem, device):
        return pltpu.make_async_remote_copy(
            src_ref=source, dst_ref=target, send_sem=send_sem, recv_sem=recv_sem, device_id=device, device_id_type=MESH
        )

    def remote(source, target, sems, index, device):
        return send(source, target, sems.at[0, index], sems.at[1, index], device)

    def total_of(terms):
        total = terms[0].astype(f32)
        for term in terms[1:]:
            total = total + term.astype(f32)
        return total

    lower = plane < 2
    middle = (plane == 1) | (plane == 2)
    order = [
        jnp.where(lower, 3, 0),
        jnp.where(plane == 0, 2, jnp.where(plane == 1, 0, jnp.where(plane == 2, 3, 1))),
        jnp.where((plane == 0) | (plane == 2), 1, 2),
        plane,
    ]
    steps = range(PLANES)
    back = [lax.rem(plane + PLANES - p, PLANES) for p in order]
    main = jnp.where(lower, 0, 1)
    main_plane = plane + 1 - 2 * main

    own_kv = [
        pltpu.make_async_copy(dkv_hbm.at[order[t], :, core], kv_own.at[t], own_sems.at[t]) for t in steps
    ] + [pltpu.make_async_copy(dq_hbm, dq_ref, own_sems.at[PLANES])]
    for copy in own_kv:
        copy.start()
    local = [
        pltpu.make_async_copy(source, target, local_sems.at[i])
        for i, (source, target) in enumerate(
            [
                (first_hbm, first),
                (joint_t_hbm, joint_t),
                (y_keep_hbm, y_keep),
                (y_got_hbm, y_got),
                (x_keep_hbm, x_keep),
                (x_got_hbm, x_got),
                (z_keep_hbm, z_keep),
                (z_got_1, z_came.at[0]),
                (z_got_2, z_came.at[1]),
                (z_got_3, z_came.at[2]),
                (tokens_hbm, tokens),
                (grad_hidden_hbm, grad_hidden),
                (joint_near_hbm, joint_near),
            ]
        )
    ]
    for i in (2, 3, 4, 5, 6, 7, 8, 9, 0, 1, 12, 10, 11):
        local[i].start()
    barrier = pltpu.get_barrier_semaphore()

    def greet(k, carry):
        pl.semaphore_signal(barrier, inc=1, device_id=(lax.rem(me + k, n), group), device_id_type=MESH)
        return carry

    lax.fori_loop(1, n, greet, 0)
    for k in range(1, groups):
        pl.semaphore_signal(barrier, inc=1, device_id=group_peer(k), device_id_type=MESH)
    pl.semaphore_wait(barrier, n - 1 + groups - 1)

    core_kv = [remote(dkv_hbm.at[order[t], :, 1 - core], kv_near.at[t], kv_sems, t, core_peer) for t in steps]
    for copy in core_kv:
        copy.start()

    per_group = joint_hbm.shape[0]
    index = me - group * per_group
    held_here = (index >= 0) & (index < per_group)
    row_own = pltpu.make_async_copy(joint_hbm.at[jnp.clip(index, 0, per_group - 1)], joint_rows, row_local.at[0])
    row_moves = [
        send(
            joint_hbm.at[jnp.clip(index, 0, per_group - 1)],
            joint_rows,
            row_sems.at[k - 1],
            row_sems.at[groups - 1],
            group_peer(k),
        )
        for k in range(1, groups)
    ]

    @pl.when(held_here)
    def _():
        row_own.start()
        for copy in row_moves:
            copy.start()

    w_moves = []

    def w_copy(source, target, device):
        copy = remote(source, target, w_sems, len(w_moves), device)
        w_moves.append(copy)
        copy.start()
        return copy

    local[2].wait()
    local[3].wait()
    for p in range(PLANES):
        for a in range(S2):
            y_keep[p, a] = total_of([y_keep[p, a]] + [y_got[k, p, a] for k in range(groups - 1)]).astype(bf)

    def z1_send(t, slot, target):
        return send(
            y_keep.at[order[t]], z1_got.at[slot], z1_sems.at[0, t], z1_sems.at[1, slot], at(target, s2, core, group)
        )

    def z1_add(t, slot):
        z1_send(0, slot, main_plane).wait_recv()
        for a in range(S2):
            y_keep[order[t], a] = total_of([y_keep[order[t], a], z1_got[slot, a]]).astype(bf)

    def z1_relay(t, slot, onward, target):
        @pl.when(middle)
        def _():
            z1_add(t, slot)
            z1_send(t, onward, target).start()

    @pl.when(jnp.logical_not(middle))
    def _():
        for t in range(PLANES - 1):
            z1_send(t, t, main_plane).start()


    def turned_back(x, t):
        cos, sin = turn_ref[back[t], :HALF], turn_ref[back[t], HALF:]
        rows = []
        for h in range(HP):
            upper, lower = x[h * HD : h * HD + HALF], x[h * HD + HALF : (h + 1) * HD]
            rows += [upper * cos + lower * sin, lower * cos - upper * sin]
        return jnp.concatenate(rows, axis=0)

    side_kv = {}
    for t in steps:
        own_kv[t].wait()
        core_kv[t].wait()
        for a in range(S2):
            kv_send[t, a] = total_of([kv_own[t, a], kv_near[t, a]]).astype(bf)
        for k in range(1, S2):
            side_kv[t, k] = remote(
                kv_send.at[t, lax.rem(s2 + S2 - k, S2)],
                kv_far.at[t, k - 1],
                kv_sems,
                PLANES + t * (S2 - 1) + k - 1,
                side_peer(S2 - k),
            )
            side_kv[t, k].start()
    own_kv[PLANES].wait()
    for t in steps:
        mixed[t, :QW] = turned_back(dq_ref[back[t]], t).astype(bf)

    local[4].wait()
    local[5].wait()
    for p in range(PLANES):
        for g in range(groups):
            x_keep[p, g] = total_of([x_keep[p, g]] + [x_got[k, p, g] for k in range(S2 - 1)]).astype(bf)
    y2 = [w_copy(x_keep.at[:, lax.rem(group + k, groups)], y2_got.at[k - 1], group_peer(k)) for k in range(1, groups)]
    for i in range(6, 10):
        local[i].wait()
    for a in range(S2):
        for g in range(groups):
            z_keep[a, g] = total_of([z_keep[a, g]] + [z_came[k, a, g] for k in range(PLANES - 1)]).astype(bf)
    y3 = [w_copy(z_keep.at[:, lax.rem(group + k, groups)], y3_got.at[k - 1], group_peer(k)) for k in range(1, groups)]

    j_moves = []

    def j_copy(source, target, device):
        copy = remote(source, target, j_sems, len(j_moves), device)
        j_moves.append(copy)
        copy.start()
        return copy

    def j_core_stage(begin, height, grads, near):
        j_acc[:height] = total_of(
            [
                jnp.dot(mixed[t, begin : begin + height], first[back[t]], preferred_element_type=f32)
                for t in steps
            ]
        )
        shard_rows = D // n
        for i in range(D // 128):
            block = j_acc[:height, i * 128 : (i + 1) * 128].T
            row = i * 128
            while row < (i + 1) * 128:
                shard, offset = divmod(row, shard_rows)
                count = min(shard_rows - offset, (i + 1) * 128 - row)
                source = row - i * 128
                grads[shard // S, shard % S // 2, shard % 2, offset : offset + count] = block[
                    source : source + count
                ].astype(bf)
                row += count
        return [j_copy(grads.at[:, :, 1 - core], near, core_peer)]

    def j_side_stage(moves, grads, near, far):
        for copy in moves:
            copy.wait()
        for p in range(PLANES):
            for a in range(S2):
                near[p, a] = total_of([grads[p, a, core], near[p, a]]).astype(bf)
        return [j_copy(near.at[:, lax.rem(s2 + k, S2)], far.at[k - 1], side_peer(k)) for k in range(1, S2)]

    def j_plane_stage(moves, near, far, gathered):
        for copy in moves:
            copy.wait()
        for p in range(PLANES):
            far[0, p] = total_of([near[p, s2]] + [far[k, p] for k in range(S2 - 1)]).astype(bf)
        gathered[plane] = far[0, plane]
        return [
            j_copy(far.at[0, lax.rem(plane + k, PLANES)], gathered.at[plane], plane_peer(k)) for k in range(1, PLANES)
        ]

    def j_group_stage(moves, gathered, every):
        for copy in moves:
            copy.wait()
        every[group] = gathered[...]
        return [j_copy(gathered, every.at[group], group_peer(k)) for k in range(1, groups)]

    local[0].wait()
    jq_moves = j_core_stage(0, QW, jq, jq_core)
    z1_relay(0, 0, 3, main_plane)

    local[1].wait()

    half = T // 2
    halves = range(2)

    def mixed_send(t, e):
        lanes = pl.ds(e * half, half)
        return send(
            mixed.at[t, :, lanes],
            mixed_got.at[t, :, lanes],
            mixed_send_sems.at[t, e],
            mixed_recv_sems.at[t, e],
            at(main_plane, s2, core, group),
        )

    def part_send(t, e, direction, target):
        rows = pl.ds(e * half, half)
        return send(
            part.at[t, rows],
            part_got.at[direction, order[t], rows],
            part_send_sems.at[t, e],
            part_recv_sems.at[direction * PLANES + order[t], e],
            at(target, s2, core, group),
        )

    def part_came(direction, p, e):
        rows = pl.ds(e * half, half)
        return send(
            part.at[0, rows],
            part_got.at[direction, p, rows],
            part_send_sems.at[0, e],
            part_recv_sems.at[direction * PLANES + p, e],
            core_peer,
        )

    other_plane = 2 * plane - main_plane

    def product(grads, columns):
        return jnp.dot(grads.T, columns, preferred_element_type=f32)

    def add_mixed(t, slot, e):
        mixed_send(slot, e).wait_recv()
        rows = slice(e * half, (e + 1) * half)
        near = product(mixed_got[slot, :, rows], joint_near[...])
        part[t, rows] = (part[t, rows].astype(f32) + near).astype(bf)

    def add_part(t, direction, p, e):
        part_came(direction, p, e).wait_recv()
        rows = slice(e * half, (e + 1) * half)
        part[t, rows] = total_of([part[t, rows], part_got[direction, p, rows]]).astype(bf)

    def relay(t, slot):
        @pl.when(middle)
        def _():
            for e in halves:
                if slot is None:
                    add_part(t, 1 - main, order[t], e)
                    part_send(t, e, 1 - main, other_plane).start()
                else:
                    add_mixed(t, slot, e)
                    part_send(t, e, main, main_plane).start()

    def key_step(t):
        for k in range(1, S2):
            side_kv[t, k].wait()
        dk = total_of([kv_send[t, s2]] + [kv_far[t, k] for k in range(S2 - 1)]).T
        mixed[t, QW : 2 * QW] = turned_back(dk[:QW], t).astype(bf)
        mixed[t, 2 * QW :] = dk[QW:].astype(bf)
        if t < PLANES - 1:

            @pl.when(jnp.logical_not(middle))
            def _():
                for e in halves:
                    mixed_send(t, e).start()

            @pl.when(middle)
            def _():
                part[t] = product(mixed[t], joint_t[: 3 * QW]).astype(bf)

        else:
            part[t] = product(mixed[t], joint_t[: 3 * QW]).astype(bf)

    local[12].wait()
    key_step(0)
    z1_relay(2, 1, 4, main_plane)
    jq_moves = j_side_stage(jq_moves, jq, jq_core, jq_side)
    key_step(1)
    z1_relay(1, 3, 5, 2 * plane - main_plane)
    for copy in y2:
        copy.wait()
    for p in range(PLANES):
        w_plane[p] = total_of([x_keep[p, group]] + [y2_got[k, p] for k in range(groups - 1)]).astype(bf)
    w_last = [
        w_copy(w_plane.at[lax.rem(plane + k, PLANES)], w_plane_got.at[k - 1], plane_peer(k)) for k in range(1, PLANES)
    ]
    key_step(2)
    relay(0, 0)
    jq_moves = j_plane_stage(jq_moves, jq_core, jq_side, jq_plane)
    key_step(3)
    relay(2, 1)
    jk_moves = j_core_stage(QW, 2 * QW, jk, jk_core)

    for copy in y3:
        copy.wait()
    for a in range(S2):
        z_keep[a, group] = total_of([z_keep[a, group]] + [y3_got[k, a] for k in range(groups - 1)]).astype(bf)
    x3 = [w_copy(z_keep.at[lax.rem(s2 + k, S2), group], x3_got.at[k - 1], side_peer(k)) for k in range(1, S2)]
    @pl.when(middle)
    def _():
        z1_add(PLANES - 1, 2)
        z1_add(PLANES - 1, 4)

    @pl.when(jnp.logical_not(middle))
    def _():
        z1_add(PLANES - 1, 5)

    x1 = [w_copy(y_keep.at[plane, lax.rem(s2 + k, S2)], x1_got.at[k - 1], side_peer(k)) for k in range(1, S2)]
    relay(1, None)
    jk_moves = j_side_stage(jk_moves, jk, jk_core, jk_side)
    jq_moves = j_group_stage(jq_moves, jq_plane, jq_all)

    local[10].wait()
    local[11].wait()
    @pl.when(middle)
    def _():
        for e in halves:
            add_mixed(PLANES - 1, 2, e)

    for e in halves:
        add_part(PLANES - 1, 1 - main, plane, e)

    strip = 64

    def norm_back(i, carry):
        rows = pl.ds(pl.multiple_of(i * strip, strip), strip)
        grad = part[PLANES - 1, rows].astype(f32)
        values = tokens[rows].astype(f32)
        centred = values - jnp.mean(values, axis=-1, keepdims=True)
        scale = lax.rsqrt(jnp.mean(centred * centred, axis=-1, keepdims=True) + norm_eps)
        normal = centred * scale
        grad = grad * gains_ref[0:1]
        grad = grad - jnp.mean(grad, axis=-1, keepdims=True) - normal * jnp.mean(grad * normal, axis=-1, keepdims=True)
        grad_hidden[rows] = grad_hidden[rows] + grad * scale
        return carry

    lax.fori_loop(0, T // strip, norm_back, 0)

    blocks = T // BLOCK
    piece = BLOCK // n

    def d_copy(source, target, base, k):
        return remote(source.at[lax.rem(me + k, n)], target.at[me], d_sems, base + k, (lax.rem(me + k, n), group))

    for i in range(n):
        d_send[i] = jnp.concatenate(
            [grad_hidden[b * BLOCK + i * piece : b * BLOCK + (i + 1) * piece] for b in range(blocks)], axis=0
        ).astype(bf)
    out_deal = [d_copy(d_send, d_mid, 0, k) for k in range(1, n)]
    for copy in out_deal:
        copy.start()
    d_mid[me] = d_send[me]

    for copy in x1 + w_last + x3:
        copy.wait()
    height = w_plane.shape[1]
    w_all[group, :height] = total_of([y_keep[plane, s2]] + [x1_got[k] for k in range(S2 - 1)]).astype(bf)
    w_all[group, height : 2 * height] = total_of(
        [w_plane[plane]] + [w_plane_got[k] for k in range(PLANES - 1)]
    ).astype(bf)
    w_all[group, 2 * height :] = total_of([z_keep[s2, group]] + [x3_got[k] for k in range(S2 - 1)]).astype(bf)
    w_gather = [w_copy(w_all.at[group], w_all.at[group], group_peer(k)) for k in range(1, groups)]
    jk_moves = j_plane_stage(jk_moves, jk_core, jk_side, jk_plane)

    for copy in out_deal:
        copy.wait()
    for i in range(n):
        chosen = []
        for b in range(blocks):
            wanted = deal_ref[i * blocks + b]
            held = d_mid[wanted // blocks].astype(f32)
            rows = held[:piece]
            for other in range(1, blocks):
                rows = jnp.where(lax.rem(wanted, blocks) == other, held[other * piece : (other + 1) * piece], rows)
            chosen.append(rows)
        d_back[i] = jnp.concatenate(chosen, axis=0).astype(bf)
    back_deal = [d_copy(d_back, d_got, n, k) for k in range(1, n)]
    for copy in back_deal:
        copy.start()
    d_got[me] = d_back[me]

    jk_moves = j_group_stage(jk_moves, jk_plane, jk_all)

    for copy in back_deal + w_gather + jq_moves + jk_moves:
        copy.wait()
    for t in range(PLANES - 1):
        z1_send(t, 0, main_plane).wait_send()
        for e in halves:

            @pl.when(middle)
            def _(t=t, e=e):
                part_send(t, e, main, main_plane).wait_send()

            @pl.when(jnp.logical_not(middle))
            def _(t=t, e=e):
                mixed_send(t, e).wait_send()

    @pl.when(held_here)
    def _():
        row_own.wait()
        for copy in row_moves:
            copy.wait_send()

    @pl.when(jnp.logical_not(held_here))
    def _():
        row_moves[0].wait_recv()


def tail(n, groups, deal, dqt, dkv, turn, gains, joint_shard, joint_t, joint_near, first, tokens, grad_hidden, pieces):
    bf, f32 = jnp.bfloat16, jnp.float32
    S2 = n // PLANES // 2
    T, D = tokens.shape
    rows = D // n
    height = pieces[0].shape[2]
    piece_rows = T // n
    joint_shard = joint_shard.reshape(-1, rows, joint_shard.shape[1])
    any_, vm, sm = (pl.BlockSpec(memory_space=m) for m in (pl.ANY, pltpu.VMEM, pltpu.SMEM))
    sems = lambda count: pltpu.SemaphoreType.DMA((2, count))
    small = lambda *s: pltpu.VMEM(s, bf)
    j_buffers = lambda w: [
        small(PLANES, S2, 2, rows, w),
        small(PLANES, S2, rows, w),
        small(S2 - 1, PLANES, rows, w),
        small(PLANES, rows, w),
    ]
    return pl.pallas_call(
        functools.partial(tail_kernel, n, groups),
        out_shape=(
            jax.ShapeDtypeStruct((n, piece_rows, D), bf),
            jax.ShapeDtypeStruct((groups, 3 * height, D), bf),
            jax.ShapeDtypeStruct((groups, PLANES, rows, QW), bf),
            jax.ShapeDtypeStruct((groups, PLANES, rows, 2 * QW), bf),
            jax.ShapeDtypeStruct(joint_shard.shape[1:], bf),
        ),
        in_specs=[sm, any_, any_, vm, vm] + [any_] * 14,
        out_specs=tuple([vm] * 4) + (any_,),
        scratch_shapes=[
            pltpu.VMEM(joint_t.shape, bf),
            pltpu.VMEM(joint_near.shape, bf),
            pltpu.VMEM((PLANES, T, D), bf),
            pltpu.VMEM((T, D), bf),
            pltpu.VMEM((T, D), f32),
            *[pltpu.VMEM(p.shape, bf) for p in pieces[:5]],
            pltpu.VMEM((PLANES - 1, *pieces[5].shape), bf),
            pltpu.SemaphoreType.DMA((13,)),
            pltpu.VMEM(dqt.shape, f32),
            small(PLANES, S2, T, 2 * QW),
            pltpu.SemaphoreType.DMA((PLANES + 1,)),
            small(PLANES, S2, T, 2 * QW),
            small(PLANES, S2, T, 2 * QW),
            small(PLANES, S2 - 1, T, 2 * QW),
            sems(PLANES * S2),
            small(PLANES, 3 * QW, T),
            small(PLANES - 1, 3 * QW, T),
            pltpu.SemaphoreType.DMA((PLANES - 1, 2)),
            pltpu.SemaphoreType.DMA((PLANES - 1, 2)),
            small(PLANES, T, D),
            small(2, PLANES, T, D),
            pltpu.SemaphoreType.DMA((PLANES - 1, 2)),
            pltpu.SemaphoreType.DMA((2 * PLANES, 2)),
            pltpu.VMEM((2 * QW, D), f32),
            *j_buffers(QW),
            *j_buffers(2 * QW),
            sems(2 * (1 + S2 - 1 + PLANES - 1 + groups - 1)),
            small(S2 - 1, height, D),
            small(groups - 1, PLANES, height, D),
            small(groups - 1, S2, height, D),
            small(6, S2, height, D),
            pltpu.SemaphoreType.DMA((2, 6)),
            small(S2 - 1, height, D),
            small(PLANES, height, D),
            small(PLANES - 1, height, D),
            sems(3 * (groups - 1) + 2 * (S2 - 1) + PLANES - 1),
            small(n, piece_rows, D),
            small(n, piece_rows, D),
            small(n, piece_rows, D),
            sems(2 * n),
            pltpu.SemaphoreType.DMA((groups,)),
            pltpu.SemaphoreType.DMA((1,)),
        ],
        compiler_params=pltpu.CompilerParams(collective_id=0, has_side_effects=True, vmem_limit_bytes=60 << 20),
    )(deal, dqt, dkv, turn, gains, joint_shard, joint_t, joint_near, first, tokens, grad_hidden, *pieces)


def finish_kernel(
    n,
    d_ref,
    w_ref,
    jq_ref,
    jk_ref,
    rows_ref,
    gains_ref,
    dealt_ref,
    joint_ref,
    output_ref,
    expand_ref,
    contract_ref,
    gain_one_ref,
    gain_two_ref,
):
    f32 = jnp.float32
    T, D = dealt_ref.shape
    blocks = T // BLOCK
    piece = BLOCK // n
    for b in range(blocks):
        for i in range(0, n, 2):
            rows = [d_ref[i + e].astype(f32)[b * piece : (b + 1) * piece] for e in range(2)]
            dealt_ref[b * BLOCK + i * piece : b * BLOCK + (i + 2) * piece] = jnp.concatenate(rows, axis=0).astype(
                dealt_ref.dtype
            )

    def summed(ref, p):
        total = ref[0, p].astype(f32)
        for g in range(1, ref.shape[0]):
            total = total + ref[g, p].astype(f32)
        return total.T

    for i in range(PLANES // 2):
        pair = [summed(jq_ref, 2 * i + e) for e in range(2)]
        joint_ref[:, i * 2 * QW : (i + 1) * 2 * QW] = jnp.concatenate(pair, axis=0).T
        pair = [summed(jk_ref, 2 * i + e) for e in range(2)]
        for part in range(2):
            cols = (part + 1) * D + i * 2 * QW
            rows = [x[part * QW : (part + 1) * QW] for x in pair]
            joint_ref[:, cols : cols + 2 * QW] = jnp.concatenate(rows, axis=0).T
    shift = D - lax.axis_index("ctx") * (D // n)

    def own_lanes(x):
        return pltpu.roll(jnp.broadcast_to(x, (8, D)), shift, 1)[0:1, : D // n]

    product = jnp.sum(joint_ref[...] * rows_ref[...].astype(f32), axis=1, keepdims=True)
    product = jnp.broadcast_to(product, (D // n, 128)).T[0:1]
    gain_one_ref[...] = product / own_lanes(gains_ref[0:1])
    height = w_ref.shape[1]
    rows = D // n
    targets = [(output_ref, 0, rows)]
    targets += [(expand_ref, i * D, rows) for i in range(expand_ref.shape[1] // D)]
    targets += [(contract_ref, 0, contract_ref.shape[0])]
    row = 0
    for target, column, count in targets:
        done = 0
        while done < count:
            g, offset = divmod(row, height)
            part = min(count - done, height - offset)
            target[done : done + part, column : column + D] = w_ref[g, offset : offset + part].astype(f32)
            done += part
            row += part
    g, offset = divmod(row, height)
    gain_two_ref[...] = own_lanes(w_ref[g, offset : offset + 1].astype(f32))


def finish(n, T, wide, contract_rows, d_got, w_all, jq_all, jk_all, joint_rows, gains):
    D = d_got.shape[-1]
    rows = D // n
    f32 = jnp.float32
    vm = pl.BlockSpec(memory_space=pltpu.VMEM)
    return pl.pallas_call(
        functools.partial(finish_kernel, n),
        out_shape=(
            jax.ShapeDtypeStruct((T, D), jnp.bfloat16),
            jax.ShapeDtypeStruct((rows, 3 * D), f32),
            jax.ShapeDtypeStruct((rows, D), f32),
            jax.ShapeDtypeStruct((rows, wide), f32),
            jax.ShapeDtypeStruct((contract_rows, D), f32),
            jax.ShapeDtypeStruct((1, rows), f32),
            jax.ShapeDtypeStruct((1, rows), f32),
        ),
        in_specs=[vm] * 6,
        out_specs=tuple([vm] * 7),
    )(d_got, w_all, jq_all, jk_all, joint_rows, gains)


def on_device(
    n,
    groups,
    tokens,
    cotangent,
    lengths,
    deal,
    joint_projection,
    output_projection,
    expand_weight,
    contract_weight,
    gain_first,
    gain_second,
):
    T, D = tokens.shape[1:]
    S = n // PLANES
    S2 = S // 2

    def over_planes(x, k):
        return lax.ppermute(x, "ctx", [(h * S + s, (h + k) % PLANES * S + s) for h in range(PLANES) for s in range(S)])

    def over_sides(x, k):
        pairs = [
            (h * S + a * 2 + c, h * S + (a + k) % S2 * 2 + c) for h in range(PLANES) for a in range(S2) for c in range(2)
        ]
        return lax.ppermute(x, "ctx", pairs)

    def over_groups(x, k):
        return lax.ppermute(x, "fsdp", [(f, (f + k) % groups) for f in range(groups)])

    def moved(x, over):
        if x.shape[0] == 1:
            return over(x, 1)
        return jnp.stack([over(x[k], k + 1) for k in range(x.shape[0])])

    first, qt, kv, joint_t, turn, gains, out_w, exp_w, con_half = front(
        n,
        groups,
        lengths,
        tokens[0],
        joint_projection,
        gain_first,
        gain_second,
        output_projection,
        expand_weight,
        contract_weight,
    )
    con_got = [over_groups(con_half, k) for k in range(1, groups)]
    out_w, exp_w = (w.reshape(-1, w.shape[-1]) for w in (out_w, exp_w))
    ot, lowt, lse = attn_fwd(n, lengths, qt, kv)
    output, grad_hidden, gt, y_keep, y_send, x_keep, x_send, z_keep, *z_send, joint_near = middle(
        n, groups, lowt, tokens[0], cotangent[0], gains, out_w, exp_w, contract_weight, joint_projection, con_got
    )
    y_got, x_got = moved(y_send, over_groups), moved(x_send, over_sides)
    z_got = [over_planes(part, k + 1) for k, part in enumerate(z_send)]
    dqt, dkv = attn_bwd(n, lengths, qt, kv, ot, lse, gt)
    d_got, w_all, jq_all, jk_all, joint_rows = tail(
        n,
        groups,
        deal[0],
        dqt,
        dkv.reshape(PLANES, S2, 2, T, 2 * QW),
        turn,
        gains,
        joint_projection,
        joint_t,
        joint_near,
        first,
        tokens[0],
        grad_hidden,
        [y_keep, y_got, x_keep, x_got, z_keep, *z_got],
    )
    dealt, shard_joint, shard_output, shard_expand, shard_contract, gain_one, gain_two = finish(
        n, T, exp_w.shape[1], contract_weight.shape[0] * groups // n, d_got, w_all, jq_all, jk_all, joint_rows, gains
    )
    return (
        output[None],
        dealt[None],
        shard_joint,
        shard_output,
        shard_expand,
        shard_contract,
        gain_one[0],
        gain_two[0],
    )


def solution(mesh):
    return jax.shard_map(
        functools.partial(on_device, mesh.shape["ctx"], mesh.shape["fsdp"]),
        mesh=mesh,
        in_specs=(
            P("fsdp", "ctx", None),
            P("fsdp", "ctx", None),
            P("fsdp", None),
            P("fsdp", None),
            P("fsdp", None),
            P("fsdp", None),
            P("fsdp", None),
            P("fsdp", None),
            P("fsdp"),
            P("fsdp"),
        ),
        out_specs=(
            P("fsdp", "ctx", None),
            P("fsdp", "ctx", None),
            P("ctx", None),
            P("ctx", None),
            P("ctx", None),
            P("ctx", None),
            P("ctx"),
            P("ctx"),
        ),
        check_vma=False,
    )
```

profile of v0, /device:TPU:0, one launch (start us, length us, event | category | flops | bytes accessed | tf_op | source)
XLA Modules:
  0.0 202.8 jit_solution(2213519053437889278)
XLA Ops:
  0.6 46.4 %shard_map.161 = (bf16[4,256,768]{2,1,0:T(8,128)(2,1)}, bf16[4,192,256]{2,1,0:T(8,128)(2,1)}, bf16[16,256,384]{2,1,0:T(8,128)(2,1)}, bf16[640,768]{1,0:T(8,128)(...) custom-call(s32[1,3]{1,0:T(1,128)} %lengths_ref.5, ...), custom_call_target="tpu_custom_call" | custom-call | tf_op jit(solution)/shard_map/pallas_call | solution.py:548
  47.0 1.6 collective-permute-start
  48.6 14.9 %shard_map.162 = (f32[4,192,256]{2,1,0:T(8,128)}, bf16[4,192,256]{2,1,0:T(8,128)(2,1)}, f32[4,8,256]{2,1,0:T(8,128)}) custom-call(s32[1,3]{1,0:T(1,128)} %lengths_ref.5, bf16[4,192,256]{2,1,0:T(8,128)(2,1)} %get-tuple-element.46.qt_ref, bf16[16,256,384]{2,1,0:T(8,128)(2,1)} %get-tuple-element.47.kv_ref), custom_call_target="tpu_custom_call" | custom-call | tf_op jit(solution)/shard_map/pallas_call | solution.py:138
  63.5 0.0 collective-permute-done.refs_0_
  63.5 0.0 copy-start.2
  63.5 0.8 copy-done.2
  64.2 31.0 %shard_map.163 = (bf16[256,768]{1,0:T(8,128)(2,1)}, f32[256,768]{1,0:T(8,128)}, bf16[4,192,256]{2,1,0:T(8,128)(2,1)}, bf16[4,2,48,768]{3,2,1,0:T(8,128)(2,1)}, b...) custom-call(bf16[4,192,256]{2,1,0:T(8,128)(2,1)} %get-tuple-element., ...), custom_call_target="tpu_custom_call" | custom-call | tf_op jit(solution)/shard_map/pallas_call | solution.py:906
  95.3 3.8 %collective-permute-start.1 = (bf16[1,4,2,48,768]{4,3,2,1,0:T(8,128)(2,1)}, bf16[1,4,2,48,768]{4,3,2,1,0:T(8,128)(2,1)S(1)}, u32[]{:S(2)}, u32[]{:S(2)}) collective-permute-start(bf16[1,4,2,48,768]{4,3,2,1,0:T(8,128)(2,1)} %get-tuple-element.65), channel_id=1, source_target_pairs={{0,1},{1,0},{2,3},{3,2},{4,5},{5,4},{6,7},{7,6},{8,9},{9,8},{10,11... | collective-permute-start | bytes 1769480 | tf_op jit(solution)/shard_map/ppermute | solution.py:1688
  99.1 0.0 collective-permute-start.2
  99.1 0.0 collective-permute-start.3
  99.1 1.8 collective-permute-start.4
  100.9 2.0 collective-permute-start.5
  102.9 22.1 %shard_map.164 = (f32[4,192,256]{2,1,0:T(8,128)}, bf16[16,256,384]{2,1,0:T(8,128)(2,1)}) custom-call(s32[1,3]{1,0:T(1,128)} %lengths_ref.5, bf16[4,192,256]{2,1,0:T(8,128)(2,1)} %get-tuple-element.46.qt_ref, bf16[16,256,384]{2,1,0:T(8,128)(2,1)} %get-tuple-element.47.kv_ref, f32[4,192,256]{2,1,0:T(8,128)} %get-tuple-element.54.ot_ref, ...), custom_call_target="tpu_custom_call" | custom-call | tf_op jit(solution)/shard_map/pallas_call | solution.py:223
  125.0 0.0 collective-permute-done.3.z_got_1
  125.0 0.0 copy-start.4
  125.0 0.0 collective-permute-done.4.z_got_2
  125.0 0.0 copy-start.5
  125.0 0.0 collective-permute-done.5.z_got_3
  125.0 0.0 copy-start.6
  125.0 0.0 collective-permute-done.1.y_got_hbm
  125.0 0.0 copy-start
  125.0 0.0 collective-permute-done.2.x_got_hbm
  125.0 0.0 copy-start.1
  125.0 0.6 copy-done.4
  125.7 0.1 copy-done.5
  125.8 0.1 copy-done.6
  125.9 0.2 copy-done
  126.1 0.2 copy-done.1
  126.3 72.5 %shard_map.165 = (bf16[16,16,768]{2,1,0:T(8,128)(2,1)}, bf16[2,144,768]{2,1,0:T(8,128)(2,1)}, bf16[2,4,48,192]{3,2,1,0:T(8,128)(2,1)}, bf16[2,4,48,384]{3,2,1,0:T(8,128)(2,1)}, bf16[48,2304]{1,0:T(8,128)(2,1)}) custom-call(s32[32]{0:T(128)} %bitcast.26, f32[4,192,256]{2,1,0:T(8,128)} %get-tuple-element.57.dq_hbm, bf16[4,2,2,256,384]{4,3,2,1,0:T(8,128)(2,1)} %bitcast.20, ...), custom_call_target="tpu_custom_call" | custom-call | tf_op jit(solution)/shard_map/pallas_call | solution.py:1513
  198.8 0.0 copy-start.3
  198.8 3.3 %shard_map.166 = (bf16[256,768]{1,0:T(8,128)(2,1)}, f32[48,2304]{1,0:T(8,128)}, f32[48,768]{1,0:T(8,128)}, f32[48,2304]{1,0:T(8,128)}, f32[72,768]{1,0:T(8,128)}, /*index=5*/f32[1,48]{1,0:T(1,128)}, f32[1,48]{1,0:T(1,128)}) custom-call(bf16[16,16,768]{2,1,0:T(8,128)(2,1)} %get-tuple-element.72.d_ref, bf16[2,144,768]{2,1,0:T(8,128)(2,1)} %get-tuple-element.73.w_ref, ...), custom_call_target="tpu_custom_call" | custom-call | tf_op jit(solution)/shard_map/pallas_call | solution.py:1644
  202.1 0.0 copy-done.3
  202.1 0.7 copy.19
Async XLA Ops:
  47.0 16.5 %collective-permute-start = (bf16[288,768]{1,0:T(8,128)(2,1)}, bf16[288,768]{1,0:T(8,128)(2,1)S(1)}, u32[]{:S(2)}, u32[]{:S(2)}) collective-permute-start(bf16[288,768]{1,0:T(8,128)(2,1)} %get-tuple-element.52), channel_id=1, source_target_pairs={{0,1},{1,0},{2,3},{3,2},{4,5},{5,4},{6,7},{7,6},{8,9},{9,8},{10,11... | collective-permute-start | bytes 1327112 | tf_op jit(solution)/shard_map/ppermute | solution.py:1688
  63.5 0.8 copy-start.2
  95.3 29.7 %collective-permute-start.1 = (bf16[1,4,2,48,768]{4,3,2,1,0:T(8,128)(2,1)}, bf16[1,4,2,48,768]{4,3,2,1,0:T(8,128)(2,1)S(1)}, u32[]{:S(2)}, u32[]{:S(2)}) collective-permute-start(bf16[1,4,2,48,768]{4,3,2,1,0:T(8,128)(2,1)} %get-tuple-element.65), channel_id=1, source_target_pairs={{0,1},{1,0},{2,3},{3,2},{4,5},{5,4},{6,7},{7,6},{8,9},{9,8},{10,11... | collective-permute-start | bytes 1769480 | tf_op jit(solution)/shard_map/ppermute | solution.py:1688
  99.1 26.0 %collective-permute-start.2 = (bf16[1,4,2,48,768]{4,3,2,1,0:T(8,128)(2,1)}, bf16[1,4,2,48,768]{4,3,2,1,0:T(8,128)(2,1)S(1)}, u32[]{:S(2)}, u32[]{:S(2)}) collective-permute-start(bf16[1,4,2,48,768]{4,3,2,1,0:T(8,128)(2,1)} %get-tuple-element.67), channel_id=1, source_target_pairs={{0,4},{2,6},{4,0},{6,2},{8,12},{10,14},{12,8},{14,10},{16,20},{18,... | collective-permute-start | bytes 1769480 | tf_op jit(solution)/shard_map/ppermute | solution.py:1685
  99.1 25.9 %collective-permute-start.3 = (bf16[2,2,48,768]{3,2,1,0:T(8,128)(2,1)}, bf16[2,2,48,768]{3,2,1,0:T(8,128)(2,1)S(1)}, u32[]{:S(2)}, u32[]{:S(2)}) collective-permute-start(bf16[2,2,48,768]{3,2,1,0:T(8,128)(2,1)} %get-tuple-element.69), channel_id=1, source_target_pairs={{0,8},{2,10},{4,12},{6,14},{8,16},{10,18},{12,20},{14,22},{16,24},... | collective-permute-start | bytes 884744 | tf_op jit(solution)/shard_map/ppermute | solution.py:1679
  99.1 25.9 %collective-permute-start.4 = (bf16[2,2,48,768]{3,2,1,0:T(8,128)(2,1)}, bf16[2,2,48,768]{3,2,1,0:T(8,128)(2,1)S(1)}, u32[]{:S(2)}, u32[]{:S(2)}) collective-permute-start(bf16[2,2,48,768]{3,2,1,0:T(8,128)(2,1)} %get-tuple-element.70), channel_id=1, source_target_pairs={{0,16},{2,18},{4,20},{6,22},{8,24},{10,26},{12,28},{14,30},{16,0},... | collective-permute-start | bytes 884744 | tf_op jit(solution)/shard_map/ppermute | solution.py:1679
  100.9 24.1 %collective-permute-start.5 = (bf16[2,2,48,768]{3,2,1,0:T(8,128)(2,1)}, bf16[2,2,48,768]{3,2,1,0:T(8,128)(2,1)S(1)}, u32[]{:S(2)}, u32[]{:S(2)}) collective-permute-start(bf16[2,2,48,768]{3,2,1,0:T(8,128)(2,1)} %get-tuple-element.71), channel_id=1, source_target_pairs={{0,24},{2,26},{4,28},{6,30},{8,0},{10,2},{12,4},{14,6},{16,8},{18,... | collective-permute-start | bytes 884744 | tf_op jit(solution)/shard_map/ppermute | solution.py:1679
  125.0 0.7 copy-start.4
  125.0 0.8 copy-start.5
  125.0 0.9 copy-start.6
  125.0 1.1 copy-start
  125.0 1.2 copy-start.1
  198.8 3.3 %copy-start.3 = (bf16[256,768]{1,0:T(8,128)(2,1)S(1)}, bf16[256,768]{1,0:T(8,128)(2,1)}, u32[]{:S(2)}) copy-start(bf16[256,768]{1,0:T(8,128)(2,1)} %get-tuple-element.53) | copy-start | bytes 1179652
where the time goes:
time: 205 us; the launch traced here: 203 us
  Pallas kernels  190 us (93%)
  starting transfers between devices  9.15 us (4%)
  local copies, waits for them, and re-layouts  2.74 us (1%)
    pallas_call x1, Pallas kernels, tail(): pl.pallas_call(functools.partial(tail_kernel, n, groups), out_shape=(jax....  72.5 us
    pallas_call x1, Pallas kernels, front(): pl.pallas_call(functools.partial(front_kernel, n, groups, lengths.shape[1...  46.4 us
    pallas_call x1, Pallas kernels, middle(): pl.pallas_call(functools.partial(middle_kernel, n, groups), out_shape=(sh...  31 us
    pallas_call x1, Pallas kernels, attn_bwd(): pl.pallas_call(functools.partial(bwd_kernel, n, lengths.shape[1]), out_sh...  22.1 us
    pallas_call x1, Pallas kernels, attn_fwd(): pl.pallas_call(functools.partial(fwd_kernel, n, lengths.shape[1]), out_sh...  14.9 us
    ppermute x2, starting transfers between devices, over_groups(): lax.ppermute(x, 'fsdp', [(f, (f + k) % groups) for f in range(groups)])  5.32 us
  transfers between devices with their start and end apart: 6, of which 0 were waited for; matrix products, arithmetic and copies ran while one was open for 0% of the time, Pallas kernels for 18%

commit v1 on v0

--- a/solution.py
+++ b/solution.py
@@ -388,7 +388,7 @@
         turn_ref[j, :HALF] = jnp.cos(angles)
         turn_ref[j, HALF:] = jnp.sin(angles)
 
-    strip = 64
+    strip = 128
 
     def kv_unit(p, a, c):
         return p * S + a * 2 + c
@@ -743,7 +743,7 @@
     attended = att[...].reshape(D, T)
     hidden[...] = tokens_ref[...].astype(f32) + jnp.dot(attended.T, out_w[...], preferred_element_type=f32)
 
-    strip = 64
+    strip = 256
 
     for copy, hand in zip(col_moves, col_hands):
         copy.wait()

time: 205 us -> 199 us (0.971)
  starting transfers between devices: 9.15 us -> 5.99 us
    ppermute x2, starting transfers between devices: 5.32 us -> 1.63 us  [over_groups(): lax.ppermute(x, 'fsdp', [(f, (f + k) % groups) for f in range(groups)])]
    pallas_call x1, Pallas kernels: 72.5 us -> 69.3 us  [tail(): pl.pallas_call(functools.partial(tail_kernel, n, groups), out_shape=(jax....]
  transfers between devices with their start and end apart: 6 -> 6, of which waited for: 0 -> 0; matrix products, arithmetic and copies ran while one was open for 0% -> 0% of each run, Pallas kernels for 18% -> 20%
where the time goes in v1:
time: 199 us; the launch traced here: 197 us
  Pallas kernels  188 us (94%)
  starting transfers between devices  5.99 us (3%)
  local copies, waits for them, and re-layouts  2.74 us (1%)
    pallas_call x1, Pallas kernels, tail(): pl.pallas_call(functools.partial(tail_kernel, n, groups), out_shape=(jax....  69.3 us
    pallas_call x1, Pallas kernels, front(): pl.pallas_call(functools.partial(front_kernel, n, groups, lengths.shape[1...  46 us
    pallas_call x1, Pallas kernels, middle(): pl.pallas_call(functools.partial(middle_kernel, n, groups), out_shape=(sh...  30.1 us
    pallas_call x1, Pallas kernels, attn_bwd(): pl.pallas_call(functools.partial(bwd_kernel, n, lengths.shape[1]), out_sh...  23.1 us
    pallas_call x1, Pallas kernels, attn_fwd(): pl.pallas_call(functools.partial(fwd_kernel, n, lengths.shape[1]), out_sh...  15.9 us
    ppermute x3, starting transfers between devices, over_planes(): lax.ppermute(x, 'ctx', [(h * S + s, (h + k) % PLANES * S + s) for h in ra...  4.29 us
  transfers between devices with their start and end apart: 6, of which 0 were waited for; matrix products, arithmetic and copies ran while one was open for 0% of the time, Pallas kernels for 20%

profile of v1, /device:TPU:0, one launch (start us, length us, event | category | flops | bytes accessed | tf_op | source)
XLA Modules:
  0.0 197.2 jit_solution(11992374432874932014)
XLA Ops:
  0.6 46.0 %shard_map.161 = (bf16[4,256,768]{2,1,0:T(8,128)(2,1)}, bf16[4,192,256]{2,1,0:T(8,128)(2,1)}, bf16[16,256,384]{2,1,0:T(8,128)(2,1)}, bf16[640,768]{1,0:T(8,128)(...) custom-call(s32[1,3]{1,0:T(1,128)} %lengths_ref.5, ...), custom_call_target="tpu_custom_call" | custom-call | tf_op jit(solution)/shard_map/pallas_call | solution.py:548
  46.7 1.6 collective-permute-start
  48.2 15.9 %shard_map.162 = (f32[4,192,256]{2,1,0:T(8,128)}, bf16[4,192,256]{2,1,0:T(8,128)(2,1)}, f32[4,8,256]{2,1,0:T(8,128)}) custom-call(s32[1,3]{1,0:T(1,128)} %lengths_ref.5, bf16[4,192,256]{2,1,0:T(8,128)(2,1)} %get-tuple-element.46.qt_ref, bf16[16,256,384]{2,1,0:T(8,128)(2,1)} %get-tuple-element.47.kv_ref), custom_call_target="tpu_custom_call" | custom-call | tf_op jit(solution)/shard_map/pallas_call | solution.py:138
  64.1 0.0 collective-permute-done.refs_0_
  64.1 0.0 copy-start.2
  64.1 0.8 copy-done.2
  64.9 30.1 %shard_map.163 = (bf16[256,768]{1,0:T(8,128)(2,1)}, f32[256,768]{1,0:T(8,128)}, bf16[4,192,256]{2,1,0:T(8,128)(2,1)}, bf16[4,2,48,768]{3,2,1,0:T(8,128)(2,1)}, b...) custom-call(bf16[4,192,256]{2,1,0:T(8,128)(2,1)} %get-tuple-element., ...), custom_call_target="tpu_custom_call" | custom-call | tf_op jit(solution)/shard_map/pallas_call | solution.py:906
  95.0 0.1 collective-permute-start.1
  95.1 0.1 collective-permute-start.2
  95.2 0.9 collective-permute-start.3
  96.1 3.4 %collective-permute-start.4 = (bf16[2,2,48,768]{3,2,1,0:T(8,128)(2,1)}, bf16[2,2,48,768]{3,2,1,0:T(8,128)(2,1)S(1)}, u32[]{:S(2)}, u32[]{:S(2)}) collective-permute-start(bf16[2,2,48,768]{3,2,1,0:T(8,128)(2,1)} %get-tuple-element.70), channel_id=1, source_target_pairs={{0,16},{2,18},{4,20},{6,22},{8,24},{10,26},{12,28},{14,30},{16,0},... | collective-permute-start | bytes 884744 | tf_op jit(solution)/shard_map/ppermute | solution.py:1679
  99.4 0.0 collective-permute-start.5
  99.4 23.1 %shard_map.164 = (f32[4,192,256]{2,1,0:T(8,128)}, bf16[16,256,384]{2,1,0:T(8,128)(2,1)}) custom-call(s32[1,3]{1,0:T(1,128)} %lengths_ref.5, bf16[4,192,256]{2,1,0:T(8,128)(2,1)} %get-tuple-element.46.qt_ref, bf16[16,256,384]{2,1,0:T(8,128)(2,1)} %get-tuple-element.47.kv_ref, f32[4,192,256]{2,1,0:T(8,128)} %get-tuple-element.54.ot_ref, ...), custom_call_target="tpu_custom_call" | custom-call | tf_op jit(solution)/shard_map/pallas_call | solution.py:223
  122.5 0.0 collective-permute-done.3.z_got_1
  122.5 0.0 copy-start.4
  122.5 0.0 collective-permute-done.4.z_got_2
  122.5 0.0 copy-start.5
  122.5 0.0 collective-permute-done.5.z_got_3
  122.6 0.0 copy-start.6
  122.6 0.0 collective-permute-done.1.y_got_hbm
  122.6 0.0 copy-start
  122.6 0.0 collective-permute-done.2.x_got_hbm
  122.6 0.0 copy-start.1
  122.6 0.6 copy-done.4
  123.2 0.1 copy-done.5
  123.3 0.1 copy-done.6
  123.4 0.2 copy-done
  123.7 0.2 copy-done.1
  123.8 69.3 %shard_map.165 = (bf16[16,16,768]{2,1,0:T(8,128)(2,1)}, bf16[2,144,768]{2,1,0:T(8,128)(2,1)}, bf16[2,4,48,192]{3,2,1,0:T(8,128)(2,1)}, bf16[2,4,48,384]{3,2,1,0:T(8,128)(2,1)}, bf16[48,2304]{1,0:T(8,128)(2,1)}) custom-call(s32[32]{0:T(128)} %bitcast.26, f32[4,192,256]{2,1,0:T(8,128)} %get-tuple-element.57.dq_hbm, bf16[4,2,2,256,384]{4,3,2,1,0:T(8,128)(2,1)} %bitcast.20, ...), custom_call_target="tpu_custom_call" | custom-call | tf_op jit(solution)/shard_map/pallas_call | solution.py:1513
  193.1 0.0 copy-start.3
  193.1 3.3 %shard_map.166 = (bf16[256,768]{1,0:T(8,128)(2,1)}, f32[48,2304]{1,0:T(8,128)}, f32[48,768]{1,0:T(8,128)}, f32[48,2304]{1,0:T(8,128)}, f32[72,768]{1,0:T(8,128)}, /*index=5*/f32[1,48]{1,0:T(1,128)}, f32[1,48]{1,0:T(1,128)}) custom-call(bf16[16,16,768]{2,1,0:T(8,128)(2,1)} %get-tuple-element.72.d_ref, bf16[2,144,768]{2,1,0:T(8,128)(2,1)} %get-tuple-element.73.w_ref, ...), custom_call_target="tpu_custom_call" | custom-call | tf_op jit(solution)/shard_map/pallas_call | solution.py:1644
  196.4 0.0 copy-done.3
  196.4 0.7 copy.19
Async XLA Ops:
  46.7 17.5 %collective-permute-start = (bf16[288,768]{1,0:T(8,128)(2,1)}, bf16[288,768]{1,0:T(8,128)(2,1)S(1)}, u32[]{:S(2)}, u32[]{:S(2)}) collective-permute-start(bf16[288,768]{1,0:T(8,128)(2,1)} %get-tuple-element.52), channel_id=1, source_target_pairs={{0,1},{1,0},{2,3},{3,2},{4,5},{5,4},{6,7},{7,6},{8,9},{9,8},{10,11... | collective-permute-start | bytes 1327112 | tf_op jit(solution)/shard_map/ppermute | solution.py:1688
  64.1 0.8 copy-start.2
  95.0 27.6 %collective-permute-start.1 = (bf16[1,4,2,48,768]{4,3,2,1,0:T(8,128)(2,1)}, bf16[1,4,2,48,768]{4,3,2,1,0:T(8,128)(2,1)S(1)}, u32[]{:S(2)}, u32[]{:S(2)}) collective-permute-start(bf16[1,4,2,48,768]{4,3,2,1,0:T(8,128)(2,1)} %get-tuple-element.65), channel_id=1, source_target_pairs={{0,1},{1,0},{2,3},{3,2},{4,5},{5,4},{6,7},{7,6},{8,9},{9,8},{10,11... | collective-permute-start | bytes 1769480 | tf_op jit(solution)/shard_map/ppermute | solution.py:1688
  95.1 27.5 %collective-permute-start.2 = (bf16[1,4,2,48,768]{4,3,2,1,0:T(8,128)(2,1)}, bf16[1,4,2,48,768]{4,3,2,1,0:T(8,128)(2,1)S(1)}, u32[]{:S(2)}, u32[]{:S(2)}) collective-permute-start(bf16[1,4,2,48,768]{4,3,2,1,0:T(8,128)(2,1)} %get-tuple-element.67), channel_id=1, source_target_pairs={{0,4},{2,6},{4,0},{6,2},{8,12},{10,14},{12,8},{14,10},{16,20},{18,... | collective-permute-start | bytes 1769480 | tf_op jit(solution)/shard_map/ppermute | solution.py:1685
  95.2 27.4 %collective-permute-start.3 = (bf16[2,2,48,768]{3,2,1,0:T(8,128)(2,1)}, bf16[2,2,48,768]{3,2,1,0:T(8,128)(2,1)S(1)}, u32[]{:S(2)}, u32[]{:S(2)}) collective-permute-start(bf16[2,2,48,768]{3,2,1,0:T(8,128)(2,1)} %get-tuple-element.69), channel_id=1, source_target_pairs={{0,8},{2,10},{4,12},{6,14},{8,16},{10,18},{12,20},{14,22},{16,24},... | collective-permute-start | bytes 884744 | tf_op jit(solution)/shard_map/ppermute | solution.py:1679
  96.1 26.5 %collective-permute-start.4 = (bf16[2,2,48,768]{3,2,1,0:T(8,128)(2,1)}, bf16[2,2,48,768]{3,2,1,0:T(8,128)(2,1)S(1)}, u32[]{:S(2)}, u32[]{:S(2)}) collective-permute-start(bf16[2,2,48,768]{3,2,1,0:T(8,128)(2,1)} %get-tuple-element.70), channel_id=1, source_target_pairs={{0,16},{2,18},{4,20},{6,22},{8,24},{10,26},{12,28},{14,30},{16,0},... | collective-permute-start | bytes 884744 | tf_op jit(solution)/shard_map/ppermute | solution.py:1679
  99.4 23.1 %collective-permute-start.5 = (bf16[2,2,48,768]{3,2,1,0:T(8,128)(2,1)}, bf16[2,2,48,768]{3,2,1,0:T(8,128)(2,1)S(1)}, u32[]{:S(2)}, u32[]{:S(2)}) collective-permute-start(bf16[2,2,48,768]{3,2,1,0:T(8,128)(2,1)} %get-tuple-element.71), channel_id=1, source_target_pairs={{0,24},{2,26},{4,28},{6,30},{8,0},{10,2},{12,4},{14,6},{16,8},{18,... | collective-permute-start | bytes 884744 | tf_op jit(solution)/shard_map/ppermute | solution.py:1679
  122.5 0.7 copy-start.4
  122.5 0.8 copy-start.5
  122.6 0.9 copy-start.6
  122.6 1.1 copy-start
  122.6 1.2 copy-start.1
  193.1 3.3 %copy-start.3 = (bf16[256,768]{1,0:T(8,128)(2,1)S(1)}, bf16[256,768]{1,0:T(8,128)(2,1)}, u32[]{:S(2)}) copy-start(bf16[256,768]{1,0:T(8,128)(2,1)} %get-tuple-element.53) | copy-start | bytes 1179652

commit v2 on v1

--- a/solution.py
+++ b/solution.py
@@ -57,11 +57,11 @@
     return (low, full_low, full_high, high), begin[0:1], end[0:1]
 
 
-def over_units(bounds, step, sizes):
+def over_units(bounds, step, sizes, masked_sizes):
     low, full_low, full_high, high = bounds
-    in_groups(low, full_low, lambda u: step(u, True), sizes[-2:])
+    in_groups(low, full_low, lambda u: step(u, True), masked_sizes)
     in_groups(full_low, full_high, lambda u: step(u, False), sizes)
-    in_groups(full_high, high, lambda u: step(u, True), sizes[-2:])
+    in_groups(full_high, high, lambda u: step(u, True), masked_sizes)
 
 
 def in_groups(begin, end, step, sizes):
@@ -106,7 +106,7 @@
                 scores[u, h] = st[h]
                 top[h] = jnp.maximum(top[h], jnp.max(st[h].reshape(T // 8, 8, T), axis=0))
 
-        over_units(bounds, score, (2, 1))
+        over_units(bounds, score, (2, 1), (2, 1))
         m = [jnp.max(top[h], axis=0, keepdims=True) for h in range(HP)]
 
         def gather(u):
@@ -201,7 +201,7 @@
                 rows = pl.ds(h * HD, HD)
                 dq[rows, :] += jnp.dot(keys[u, rows, :], ds[h], preferred_element_type=jnp.float32)
 
-        over_units(bounds, one_unit, (4, 2, 1))
+        over_units(bounds, one_unit, (4, 2, 1), (4, 2, 1))
         dqt_ref[b] = dq[...] * (HD**-0.5)
         return carry
 
@@ -388,7 +388,7 @@
         turn_ref[j, :HALF] = jnp.cos(angles)
         turn_ref[j, HALF:] = jnp.sin(angles)
 
-    strip = 128
+    strip = 256
 
     def kv_unit(p, a, c):
         return p * S + a * 2 + c

time: 199 us -> 199 us (level); the launches traced: 197 us -> 201 us
  starting transfers between devices: 5.99 us -> 9.22 us
    ppermute x2, starting transfers between devices: 1.63 us -> 5.39 us  [over_groups(): lax.ppermute(x, 'fsdp', [(f, (f + k) % groups) for f in range(groups)])]
    pallas_call x1, Pallas kernels: 69.3 us -> 72.8 us  [tail(): pl.pallas_call(functools.partial(tail_kernel, n, groups), out_shape=(jax....]
  transfers between devices with their start and end apart: 6 -> 6, of which waited for: 0 -> 0; matrix products, arithmetic and copies ran while one was open for 0% -> 0% of each run, Pallas kernels for 20% -> 18%
where the time goes in v2:
time: 199 us; the launch traced here: 201 us
  Pallas kernels  188 us (94%)
  starting transfers between devices  9.22 us (5%)
  local copies, waits for them, and re-layouts  2.74 us (1%)
    pallas_call x1, Pallas kernels, tail(): pl.pallas_call(functools.partial(tail_kernel, n, groups), out_shape=(jax....  72.8 us
    pallas_call x1, Pallas kernels, front(): pl.pallas_call(functools.partial(front_kernel, n, groups, lengths.shape[1...  45.8 us
    pallas_call x1, Pallas kernels, middle(): pl.pallas_call(functools.partial(middle_kernel, n, groups), out_shape=(sh...  29.4 us
    pallas_call x1, Pallas kernels, attn_bwd(): pl.pallas_call(functools.partial(bwd_kernel, n, lengths.shape[1]), out_sh...  22 us
    pallas_call x1, Pallas kernels, attn_fwd(): pl.pallas_call(functools.partial(fwd_kernel, n, lengths.shape[1]), out_sh...  14.9 us
    ppermute x2, starting transfers between devices, over_groups(): lax.ppermute(x, 'fsdp', [(f, (f + k) % groups) for f in range(groups)])  5.39 us
  transfers between devices with their start and end apart: 6, of which 0 were waited for; matrix products, arithmetic and copies ran while one was open for 0% of the time, Pallas kernels for 18%

profile of v2, /device:TPU:0, one launch (start us, length us, event | category | flops | bytes accessed | tf_op | source)
XLA Modules:
  0.0 200.9 jit_solution(17338223819426080026)
XLA Ops:
  0.6 45.8 %shard_map.161 = (bf16[4,256,768]{2,1,0:T(8,128)(2,1)}, bf16[4,192,256]{2,1,0:T(8,128)(2,1)}, bf16[16,256,384]{2,1,0:T(8,128)(2,1)}, bf16[640,768]{1,0:T(8,128)(...) custom-call(s32[1,3]{1,0:T(1,128)} %lengths_ref.5, ...), custom_call_target="tpu_custom_call" | custom-call | tf_op jit(solution)/shard_map/pallas_call | solution.py:548
  46.5 1.6 collective-permute-start
  48.0 14.9 %shard_map.162 = (f32[4,192,256]{2,1,0:T(8,128)}, bf16[4,192,256]{2,1,0:T(8,128)(2,1)}, f32[4,8,256]{2,1,0:T(8,128)}) custom-call(s32[1,3]{1,0:T(1,128)} %lengths_ref.5, bf16[4,192,256]{2,1,0:T(8,128)(2,1)} %get-tuple-element.46.qt_ref, bf16[16,256,384]{2,1,0:T(8,128)(2,1)} %get-tuple-element.47.kv_ref), custom_call_target="tpu_custom_call" | custom-call | tf_op jit(solution)/shard_map/pallas_call | solution.py:138
  62.9 0.0 collective-permute-done.refs_0_
  62.9 0.0 copy-start.2
  62.9 0.8 copy-done.2
  63.7 29.4 %shard_map.163 = (bf16[256,768]{1,0:T(8,128)(2,1)}, f32[256,768]{1,0:T(8,128)}, bf16[4,192,256]{2,1,0:T(8,128)(2,1)}, bf16[4,2,48,768]{3,2,1,0:T(8,128)(2,1)}, b...) custom-call(bf16[4,192,256]{2,1,0:T(8,128)(2,1)} %get-tuple-element., ...), custom_call_target="tpu_custom_call" | custom-call | tf_op jit(solution)/shard_map/pallas_call | solution.py:906
  93.1 3.8 %collective-permute-start.1 = (bf16[1,4,2,48,768]{4,3,2,1,0:T(8,128)(2,1)}, bf16[1,4,2,48,768]{4,3,2,1,0:T(8,128)(2,1)S(1)}, u32[]{:S(2)}, u32[]{:S(2)}) collective-permute-start(bf16[1,4,2,48,768]{4,3,2,1,0:T(8,128)(2,1)} %get-tuple-element.65), channel_id=1, source_target_pairs={{0,1},{1,0},{2,3},{3,2},{4,5},{5,4},{6,7},{7,6},{8,9},{9,8},{10,11... | collective-permute-start | bytes 1769480 | tf_op jit(solution)/shard_map/ppermute | solution.py:1688
  96.9 0.0 collective-permute-start.2
  96.9 0.0 collective-permute-start.3
  96.9 1.8 collective-permute-start.4
  98.7 2.0 %collective-permute-start.5 = (bf16[2,2,48,768]{3,2,1,0:T(8,128)(2,1)}, bf16[2,2,48,768]{3,2,1,0:T(8,128)(2,1)S(1)}, u32[]{:S(2)}, u32[]{:S(2)}) collective-permute-start(bf16[2,2,48,768]{3,2,1,0:T(8,128)(2,1)} %get-tuple-element.71), channel_id=1, source_target_pairs={{0,24},{2,26},{4,28},{6,30},{8,0},{10,2},{12,4},{14,6},{16,8},{18,... | collective-permute-start | bytes 884744 | tf_op jit(solution)/shard_map/ppermute | solution.py:1679
  100.8 22.0 %shard_map.164 = (f32[4,192,256]{2,1,0:T(8,128)}, bf16[16,256,384]{2,1,0:T(8,128)(2,1)}) custom-call(s32[1,3]{1,0:T(1,128)} %lengths_ref.5, bf16[4,192,256]{2,1,0:T(8,128)(2,1)} %get-tuple-element.46.qt_ref, bf16[16,256,384]{2,1,0:T(8,128)(2,1)} %get-tuple-element.47.kv_ref, f32[4,192,256]{2,1,0:T(8,128)} %get-tuple-element.54.ot_ref, ...), custom_call_target="tpu_custom_call" | custom-call | tf_op jit(solution)/shard_map/pallas_call | solution.py:223
  122.8 0.0 collective-permute-done.3.z_got_1
  122.8 0.0 copy-start.4
  122.8 0.0 collective-permute-done.4.z_got_2
  122.8 0.0 copy-start.5
  122.8 0.0 collective-permute-done.5.z_got_3
  122.8 0.0 copy-start.6
  122.8 0.0 collective-permute-done.1.y_got_hbm
  122.8 0.0 copy-start
  122.8 0.0 collective-permute-done.2.x_got_hbm
  122.8 0.0 copy-start.1
  122.9 0.6 copy-done.4
  123.5 0.1 copy-done.5
  123.6 0.1 copy-done.6
  123.7 0.2 copy-done
  123.9 0.2 copy-done.1
  124.1 72.8 %shard_map.165 = (bf16[16,16,768]{2,1,0:T(8,128)(2,1)}, bf16[2,144,768]{2,1,0:T(8,128)(2,1)}, bf16[2,4,48,192]{3,2,1,0:T(8,128)(2,1)}, bf16[2,4,48,384]{3,2,1,0:T(8,128)(2,1)}, bf16[48,2304]{1,0:T(8,128)(2,1)}) custom-call(s32[32]{0:T(128)} %bitcast.26, f32[4,192,256]{2,1,0:T(8,128)} %get-tuple-element.57.dq_hbm, bf16[4,2,2,256,384]{4,3,2,1,0:T(8,128)(2,1)} %bitcast.20, ...), custom_call_target="tpu_custom_call" | custom-call | tf_op jit(solution)/shard_map/pallas_call | solution.py:1513
  196.9 0.0 copy-start.3
  196.9 3.3 %shard_map.166 = (bf16[256,768]{1,0:T(8,128)(2,1)}, f32[48,2304]{1,0:T(8,128)}, f32[48,768]{1,0:T(8,128)}, f32[48,2304]{1,0:T(8,128)}, f32[72,768]{1,0:T(8,128)}, /*index=5*/f32[1,48]{1,0:T(1,128)}, f32[1,48]{1,0:T(1,128)}) custom-call(bf16[16,16,768]{2,1,0:T(8,128)(2,1)} %get-tuple-element.72.d_ref, bf16[2,144,768]{2,1,0:T(8,128)(2,1)} %get-tuple-element.73.w_ref, ...), custom_call_target="tpu_custom_call" | custom-call | tf_op jit(solution)/shard_map/pallas_call | solution.py:1644
  200.2 0.0 copy-done.3
  200.2 0.7 copy.19
Async XLA Ops:
  46.5 16.5 %collective-permute-start = (bf16[288,768]{1,0:T(8,128)(2,1)}, bf16[288,768]{1,0:T(8,128)(2,1)S(1)}, u32[]{:S(2)}, u32[]{:S(2)}) collective-permute-start(bf16[288,768]{1,0:T(8,128)(2,1)} %get-tuple-element.52), channel_id=1, source_target_pairs={{0,1},{1,0},{2,3},{3,2},{4,5},{5,4},{6,7},{7,6},{8,9},{9,8},{10,11... | collective-permute-start | bytes 1327112 | tf_op jit(solution)/shard_map/ppermute | solution.py:1688
  62.9 0.8 copy-start.2
  93.1 29.7 %collective-permute-start.1 = (bf16[1,4,2,48,768]{4,3,2,1,0:T(8,128)(2,1)}, bf16[1,4,2,48,768]{4,3,2,1,0:T(8,128)(2,1)S(1)}, u32[]{:S(2)}, u32[]{:S(2)}) collective-permute-start(bf16[1,4,2,48,768]{4,3,2,1,0:T(8,128)(2,1)} %get-tuple-element.65), channel_id=1, source_target_pairs={{0,1},{1,0},{2,3},{3,2},{4,5},{5,4},{6,7},{7,6},{8,9},{9,8},{10,11... | collective-permute-start | bytes 1769480 | tf_op jit(solution)/shard_map/ppermute | solution.py:1688
  96.9 25.9 %collective-permute-start.2 = (bf16[1,4,2,48,768]{4,3,2,1,0:T(8,128)(2,1)}, bf16[1,4,2,48,768]{4,3,2,1,0:T(8,128)(2,1)S(1)}, u32[]{:S(2)}, u32[]{:S(2)}) collective-permute-start(bf16[1,4,2,48,768]{4,3,2,1,0:T(8,128)(2,1)} %get-tuple-element.67), channel_id=1, source_target_pairs={{0,4},{2,6},{4,0},{6,2},{8,12},{10,14},{12,8},{14,10},{16,20},{18,... | collective-permute-start | bytes 1769480 | tf_op jit(solution)/shard_map/ppermute | solution.py:1685
  96.9 25.8 %collective-permute-start.3 = (bf16[2,2,48,768]{3,2,1,0:T(8,128)(2,1)}, bf16[2,2,48,768]{3,2,1,0:T(8,128)(2,1)S(1)}, u32[]{:S(2)}, u32[]{:S(2)}) collective-permute-start(bf16[2,2,48,768]{3,2,1,0:T(8,128)(2,1)} %get-tuple-element.69), channel_id=1, source_target_pairs={{0,8},{2,10},{4,12},{6,14},{8,16},{10,18},{12,20},{14,22},{16,24},... | collective-permute-start | bytes 884744 | tf_op jit(solution)/shard_map/ppermute | solution.py:1679
  96.9 25.9 %collective-permute-start.4 = (bf16[2,2,48,768]{3,2,1,0:T(8,128)(2,1)}, bf16[2,2,48,768]{3,2,1,0:T(8,128)(2,1)S(1)}, u32[]{:S(2)}, u32[]{:S(2)}) collective-permute-start(bf16[2,2,48,768]{3,2,1,0:T(8,128)(2,1)} %get-tuple-element.70), channel_id=1, source_target_pairs={{0,16},{2,18},{4,20},{6,22},{8,24},{10,26},{12,28},{14,30},{16,0},... | collective-permute-start | bytes 884744 | tf_op jit(solution)/shard_map/ppermute | solution.py:1679
  98.7 24.1 %collective-permute-start.5 = (bf16[2,2,48,768]{3,2,1,0:T(8,128)(2,1)}, bf16[2,2,48,768]{3,2,1,0:T(8,128)(2,1)S(1)}, u32[]{:S(2)}, u32[]{:S(2)}) collective-permute-start(bf16[2,2,48,768]{3,2,1,0:T(8,128)(2,1)} %get-tuple-element.71), channel_id=1, source_target_pairs={{0,24},{2,26},{4,28},{6,30},{8,0},{10,2},{12,4},{14,6},{16,8},{18,... | collective-permute-start | bytes 884744 | tf_op jit(solution)/shard_map/ppermute | solution.py:1679
  122.8 0.7 copy-start.4
  122.8 0.8 copy-start.5
  122.8 0.9 copy-start.6
  122.8 1.1 copy-start
  122.8 1.2 copy-start.1
  196.9 3.3 %copy-start.3 = (bf16[256,768]{1,0:T(8,128)(2,1)S(1)}, bf16[256,768]{1,0:T(8,128)(2,1)}, u32[]{:S(2)}) copy-start(bf16[256,768]{1,0:T(8,128)(2,1)} %get-tuple-element.53) | copy-start | bytes 1179652
